TPU v7x, 256 devices: a whole 4x4x8 slice. The times are simulated.
256 devices in a mesh: gx: 128 (over x, y, z), gy: 2 (over core).
Axes of the slice: x: 4, y: 4, z: 8, core: 2. Of those that a mesh axis runs over, the one named last changes fastest.
Arguments:
- embeddings: bfloat16 [114688, 1024], P(('gx', 'gy')), may hold values from -16 to 16
- cluster: int32 [114688, 1], P(('gx', 'gy')), may hold values from 0 to 127; in each aligned block of 448 rows (0 to 447, 448 to 895, ...) at most 7 rows name the same one
Outputs:
- density: float32 [114688], P(('gx', 'gy'))
Inputs may be any that keep to these rules, and one draw needn't show every extreme that they name: Within each aligned block of 448 rows (the rows of one device) no cluster id appears more than 7 times, and some id appears exactly 7 times.
All inputs are finite; a program needn't handle non-finite values.
Results may differ from a plain program's by a relative error of at most 0.0003.
Values may be sent and summed in bfloat16 or wider, within the bound.
No kernel may reach another device: no remote copies, remote signals or barrier semaphores. Data moves between devices by JAX's collectives and lax.ppermute only.
A program may use at most 64 MiB of HBM per device.

v0:
```python
import math

import jax
import jax.numpy as jnp
from jax import lax
from jax.sharding import PartitionSpec as P

D = 1024


prior_score = math.log(64.0)


def side_by_side(arrays, axis, split_dim, concat_dim, along):
    columns = [a.reshape(*a.shape[:along], -1) for a in arrays]
    both = jnp.concatenate(columns, axis=along)
    filled, at, outs = (
        lax.all_to_all(both, axis, split_axis=split_dim, concat_axis=concat_dim, tiled=True),
        0,
        [],
    )
    for a, column in zip(arrays, columns):
        section = filled[..., at : at + column.shape[along]]
        outs.append(section.reshape(*section.shape[:along], *a.shape[along:]))
        at += column.shape[along]
    return tuple(outs)


def from_partner(value, axis, bit):
    mask = 2**bit
    pairs = [(source, source ^ mask) for source in range(lax.axis_size(axis))]
    return lax.ppermute(value, axis, pairs)


def fold_block(running, own_rows, key_rows, key_flags, key_index, query_index):
    peak_now, total_now = running
    scores = jnp.einsum(
        "qd,kd->qk", own_rows, key_rows, preferred_element_type=jnp.float32
    ) * D ** (-0.5)
    key_mask = (key_flags[None, :] > 0.5) & (key_index[None, :] != query_index[:, None])
    shifted = jnp.where(key_mask, scores, prior_score)
    peak_next = jnp.maximum(peak_now, jnp.max(shifted, axis=1))
    terms = jnp.where(key_mask, jnp.exp(shifted - peak_next[:, None]), 0.0)
    total_next = total_now * jnp.exp(peak_now - peak_next) + jnp.sum(terms, axis=1)
    return (peak_next, total_next)


def shards(embeddings, cluster):
    owners = lax.axis_size("gx")
    row_count = embeddings.shape[0]
    width = embeddings.shape[1]
    capacity = 2 * row_count // owners
    slot_count = owners * capacity
    cluster_ids = cluster[:, 0]
    onehot = (cluster_ids[:, None] == jnp.arange(owners, dtype=jnp.int32)[None, :]).astype(
        jnp.int32
    )
    member_rank = jnp.sum(jnp.cumsum(onehot, axis=0) * onehot, axis=1) - 1
    slot_index = cluster_ids * capacity + member_rank
    send_rows = jnp.zeros((slot_count, width), jnp.bfloat16).at[slot_index].set(embeddings)
    send_flags = (
        jnp.zeros((slot_count,), jnp.bfloat16)
        .at[slot_index]
        .set(jnp.ones((row_count,), jnp.bfloat16))
    )
    recv_rows, recv_flags = side_by_side(
        (send_rows.reshape(owners, capacity, width), send_flags.reshape(owners, capacity)),
        "gx",
        0,
        0,
        2,
    )
    own_rows = recv_rows.reshape(slot_count, width)
    own_flags = recv_flags.reshape(slot_count)
    slot_range = jnp.arange(slot_count, dtype=jnp.int32)
    query_index = lax.axis_index("gy") * slot_count + slot_range
    initial = (
        jnp.full((slot_count,), prior_score, jnp.float32),
        jnp.ones((slot_count,), jnp.float32),
    )
    other_rows, other_flags = from_partner((own_rows, own_flags), "gy", 0)
    other_index = (1 - lax.axis_index("gy")) * slot_count + slot_range
    key_rows = jnp.concatenate([own_rows, other_rows], axis=0)
    key_flags = jnp.concatenate([own_flags, other_flags], axis=0)
    key_index = jnp.concatenate([query_index, other_index], axis=0)
    peak, total = fold_block(initial, own_rows, key_rows, key_flags, key_index, query_index)
    density_slots = peak + jnp.log(total)
    returned = lax.all_to_all(
        density_slots.reshape(owners, capacity), "gx", split_axis=0, concat_axis=0, tiled=True
    )
    return returned.reshape(slot_count)[slot_index]


def solution(mesh):
    return jax.shard_map(
        shards,
        mesh=mesh,
        in_specs=(P(("gx", "gy"), None), P(("gx", "gy"), None)),
        out_specs=P(("gx", "gy")),
        check_vma=False,
    )
```

profile of v0, /device:TPU:1, one launch (start us, length us, event | category | flops | bytes accessed | tf_op | source)
XLA Modules:
  0.0 137.4 jit_solution(607669577872950049)
XLA Ops:
  0.0 0.8 iota_compare_fusion
  1.1 0.9 fusion.9
  2.1 0.7 compare_select_fusion
  2.7 4.4 %scatter_custom_fusion = bf16[896,1024]{1,0:T(8,128)(2,1)} fusion(s32[448]{0:T(512)S(1)} %bitcast.21, bf16[448,1024]{1,0:T(8,128)(2,1)} %param.2, bf16[]{:T(256)} %constant.14.clone.1), kind=kCustom, calls=%fused_computation.12 | custom fusion | bytes 1835520 | tf_op jit(solution)/shard_map/scatter | solution.py:60
  7.1 2.6 %reshape.96 = bf16[128,7,1024]{2,1,0:T(8,128)(2,1)S(1)} reshape(bf16[896,1024]{1,0:T(8,128)(2,1)} %scatter_custom_fusion) | data formatting | bytes 3670016 | tf_op jit(solution)/shard_map/reshape | solution.py:67
  9.8 3.4 %scatter_custom_fusion.1 = bf16[896]{0:T(1024)(128)(2,1)S(1)} fusion(s32[448]{0:T(512)S(1)} %bitcast.22, bf16[448]{0:T(512)(128)(2,1)S(1)} %broadcast.69, bf16[]{:T(256)} %constant.14.clone.1), kind=kCustom, calls=%fused_computation.32 | custom fusion | bytes 1794 | tf_op jit(solution)/shard_map/scatter | solution.py:64
  13.1 0.3 reshape_reshape.5
  13.4 0.5 pad_maximum_fusion
  14.0 74.4 %all_to_all.11 = bf16[128,7,1025]{2,1,0:T(8,128)(2,1)S(1)} all-to-all(bf16[128,7,1025]{2,1,0:T(8,128)(2,1)S(1)} %pad_maximum_fusion), channel_id=1, replica_groups=mesh['gx'=128,'gy'=2] {'gx'}, dimensions={0} | all-to-all | bytes 3673600 | tf_op jit(solution)/shard_map/all_to_all | solution.py:18
  88.4 1.7 %slice.25 = bf16[128,7,1024]{2,1,0:T(8,128)(2,1)} slice(bf16[128,7,1025]{2,1,0:T(8,128)(2,1)S(1)} %all_to_all.11), slice={[0:128], [0:7], [0:1024]} | slice | bytes 3670016 | tf_op jit(solution)/shard_map/slice | solution.py:23
  90.1 3.9 %reshape.97 = bf16[896,1024]{1,0:T(8,128)(2,1)} reshape(bf16[128,7,1024]{2,1,0:T(8,128)(2,1)} %slice.25) | data formatting | bytes 3670016 | tf_op jit(solution)/shard_map/reshape | solution.py:73
  93.9 2.6 %collective-permute-start.1 = (bf16[896,1024]{1,0:T(8,128)(2,1)}, bf16[896,1024]{1,0:T(8,128)(2,1)}, u32[]{:S(2)}, u32[]{:S(2)}) collective-permute-start(bf16[896,1024]{1,0:T(8,128)(2,1)} %reshape.97), channel_id=1, source_target_pairs={{0,1},{1,0},{2,3},{3,2},{4,5},{5,4},{6,7},{7,6},{8,9},{9,8},{10,11... | collective-permute-start | bytes 5505032 | tf_op jit(solution)/shard_map/ppermute | solution.py:32
  96.6 0.2 slice_reduce_fusion
  96.8 0.2 concatenate.19
  97.0 0.3 collective-permute-start
  97.3 3.0 %collective-permute-done = bf16[896]{0:T(1024)(128)(2,1)S(1)} collective-permute-done((bf16[896]{0:T(1024)(128)(2,1)S(1)}, bf16[896]{0:T(1024)(128)(2,1)S(1)}, u32[]{:S(2)}, u32[]{:S(2)}) %collective-permute-start) | collective-permute-done | bytes 1824 | tf_op jit(solution)/shard_map/ppermute | solution.py:32
  100.3 9.1 %fusion = (f32[896]{0:T(1024)S(1)}, f32[896,1792]{1,0:T(8,128)}) fusion(s32[1792]{0:T(1024)S(1)} %pad_add_fusion, s32[896]{0:T(1024)S(1)} %get-tuple-element.8, pred[1792]{0:T(1024)(128)(4,1)S(1)} %maximum_compare_fusion, bf16[896,1024]{1,0:T(8,128)(2,1)} %reshape.97, bf16[896,1024]{1,0:T(8,128)(2,1)} %collective-permute-done.1), kind=kOutput, calls=%fused_computation.6 | convolution fusion | flops 3303701504 | bytes 10108672 | tf_op jit(solution)/shard_map/qd,kd->qk/dot_general | solution.py:37
  109.7 5.3 %select_reduce_fusion = f32[896]{0:T(1024)S(1)} fusion(f32[896,1792]{1,0:T(8,128)} %get-tuple-element.6, f32[896]{0:T(1024)S(1)} %broadcast_maximum_fusion, s32[1792]{0:T(1024)S(1)} %pad_add_fusion, s32[896]{0:T(1024)S(1)} %get-tuple-element.8, pred[1792]{0:T(1024)(128)(4,1)S(1)} %maximum_compare_fusion), kind=kLoop, calls=%fused_computation.3 | loop fusion | flops 11238528 | bytes 6442240 | tf_op jit(solution)/shard_map/reduce_sum | solution.py:44
  115.2 0.7 log_add_fusion
  115.8 6.2 %all-to-all-start.1 = ((f32[128,1,7]{2,1,0:T(1,128)}), f32[128,1,7]{2,1,0:T(1,128)S(1)}, u32[]{:S(2)}, u32[]{:S(2)}) async-start(f32[128,1,7]{2,1,0:T(1,128)} %bitcast.7), calls=%async_computation.1 | async-start | bytes 131072 | tf_op jit(solution)/shard_map/all_to_all | solution.py:88
  122.0 10.6 %all-to-all-done.1 = f32[128,1,7]{2,1,0:T(1,128)S(1)} async-done(((f32[128,1,7]{2,1,0:T(1,128)}), f32[128,1,7]{2,1,0:T(1,128)S(1)}, u32[]{:S(2)}, u32[]{:S(2)}) %all-to-all-start.1) | async-done | bytes 3616 | tf_op jit(solution)/shard_map/all_to_all | solution.py:88
  132.6 0.5 broadcast.83
  133.1 0.8 reduce.5
  134.1 3.2 %gather_fusion = f32[448]{0:T(512)} fusion(f32[896]{0:T(1024)S(1)} %reshape.98, s32[1024]{0:T(1024)S(1)} %pad_clamp_fusion), kind=kCustom, calls=%fused_computation | custom fusion | bytes 5376 | tf_op jit(solution)/shard_map/gather | solution.py:91
  (19 shorter events, 0.9 us)
Async XLA Ops:
  93.9 6.4 %collective-permute-start.1 = (bf16[896,1024]{1,0:T(8,128)(2,1)}, bf16[896,1024]{1,0:T(8,128)(2,1)}, u32[]{:S(2)}, u32[]{:S(2)}) collective-permute-start(bf16[896,1024]{1,0:T(8,128)(2,1)} %reshape.97), channel_id=1, source_target_pairs={{0,1},{1,0},{2,3},{3,2},{4,5},{5,4},{6,7},{7,6},{8,9},{9,8},{10,11... | collective-permute-start | bytes 5505032 | tf_op jit(solution)/shard_map/ppermute | solution.py:32
  97.0 3.3 %collective-permute-start = (bf16[896]{0:T(1024)(128)(2,1)S(1)}, bf16[896]{0:T(1024)(128)(2,1)S(1)}, u32[]{:S(2)}, u32[]{:S(2)}) collective-permute-start(bf16[896]{0:T(1024)(128)(2,1)S(1)} %concatenate.19), channel_id=1, source_target_pairs={{0,1},{1,0},{2,3},{3,2},{4,5},{5,4},{6,7},{7,6},{8,9},{9,8},{10,11... | collective-permute-start | bytes 5384 | tf_op jit(solution)/shard_map/ppermute | solution.py:32
  115.8 16.8 %all-to-all-start.1 = ((f32[128,1,7]{2,1,0:T(1,128)}), f32[128,1,7]{2,1,0:T(1,128)S(1)}, u32[]{:S(2)}, u32[]{:S(2)}) async-start(f32[128,1,7]{2,1,0:T(1,128)} %bitcast.7), calls=%async_computation.1 | async-start | bytes 131072 | tf_op jit(solution)/shard_map/all_to_all | solution.py:88
where the time goes:
time: 138 us; the launch traced here: 137 us
  blocking collectives  74.4 us (54%)
  local copies, waits for them, and re-layouts  21 us (15%)
  waiting for transfers between devices  13.6 us (10%)
  other arithmetic  9.97 us (7%)
  matrix products  9.14 us (7%)
  starting transfers between devices  9.09 us (7%)
    all_to_all x1, blocking collectives, side_by_side(): lax.all_to_all(both, axis, split_axis=split_dim, concat_axis=concat_dim,...  74.4 us
    all_to_all x1, waiting for transfers between devices, shards(): lax.all_to_all(density_slots.reshape(owners, capacity), 'gx', split_axis=...  10.6 us
    dot_general x1, matrix products, fold_block(): jnp.einsum('qd,kd->qk', own_rows, key_rows, preferred_element_type=jnp.fl...  9.14 us
    all_to_all x1, starting transfers between devices, shards(): lax.all_to_all(density_slots.reshape(owners, capacity), 'gx', split_axis=...  6.17 us
    reduce_sum x1, other arithmetic, fold_block(): jnp.sum(terms, axis=1)  5.28 us
    scatter x1, local copies, waits for them, and re-layouts, shards(): jnp.zeros((slot_count, width), jnp.bfloat16).at[slot_index].set(embeddings)  4.4 us
    reshape x1, local copies, waits for them, and re-layouts, shards(): own_rows = recv_rows.reshape(slot_count, width)  3.86 us
    scatter x1, local copies, waits for them, and re-layouts, shards(): send_flags = jnp.zeros((slot_count,), jnp.bfloat16).at[slot_index].set(jn...  3.36 us
  transfers between devices with their start and end apart: 3, of which 2 were waited for; matrix products, arithmetic and copies ran while one was open for 0% of the time, Pallas kernels for 0%

commit v1 on v0

v1 whole, which is shorter than its diff:
```python
import math

import jax
import jax.numpy as jnp
from jax import lax
from jax.experimental import pallas as pl
from jax.experimental.pallas import tpu as pltpu
from jax.sharding import PartitionSpec as P

prior_score = math.log(64.0)
ABSENT = 32.0
HIDDEN = -1e30
LANES = 128
SLOTS = 8


def iota(shape, dim):
    return lax.broadcasted_iota(jnp.int32, shape, dim)


def whole(shape):
    return pl.BlockSpec(shape, lambda: (0,) * len(shape))


def dot(a, b):
    return jnp.dot(a, b, preferred_element_type=jnp.float32)


def dot_t(a, b):
    return lax.dot_general(a, b, (((1,), (1,)), ((), ())), preferred_element_type=jnp.float32)


def pack_kernel(cluster_ref, rows_ref, send_ref, slot_ref):
    row_count, width = rows_ref.shape
    owners = send_ref.shape[0] // SLOTS
    main = width - LANES
    ids = cluster_ref[...]
    owner = iota((owners, row_count), 0)
    named = owner == ids
    before = (iota((row_count, row_count), 0) < iota((row_count, row_count), 1)).astype(jnp.bfloat16)
    earlier = dot(named.astype(jnp.bfloat16), before)
    rank = jnp.sum(jnp.where(named, earlier, 0.0), axis=0, keepdims=True).astype(jnp.int32)
    slot = ids * SLOTS + rank
    slot_ref[...] = slot
    place = iota((owners * SLOTS, row_count), 0) == slot
    place_f = place.astype(jnp.float32)
    filled = jnp.sum(place_f, axis=1, keepdims=True)
    place_b = place_f.astype(jnp.bfloat16)
    slots = dot(place_b, rows_ref[:, :main])
    lane = iota((owners * SLOTS, LANES), 1)
    level = iota((owners * SLOTS, LANES), 0) % SLOTS
    last = level == SLOTS - 1
    for j in range(main // LANES):
        chunk = slots[:, j * LANES : (j + 1) * LANES]
        if j == 0:
            chunk = jnp.where((lane == 0) & (filled == 0.0), ABSENT, chunk)
        here = (owner * SLOTS + j == slot).astype(jnp.bfloat16)
        rest = dot(here, rows_ref[:, main:])
        rest = jnp.broadcast_to(rest[:, None, :], (owners, SLOTS, LANES)).reshape(owners * SLOTS, LANES)
        chunk = jnp.where(last, rest, chunk)
        send_ref[:, j * LANES : (j + 1) * LANES] = chunk.astype(jnp.bfloat16)


def pack(ids, rows):
    row_count, width = rows.shape
    owners = LANES
    return pl.pallas_call(
        pack_kernel,
        out_shape=(
            jax.ShapeDtypeStruct((owners * SLOTS, width - LANES), jnp.bfloat16),
            jax.ShapeDtypeStruct((1, row_count), jnp.int32),
        ),
        name="pack",
    )(ids, rows)


def full_rows(got_ref, full_ref):
    count, main = got_ref.shape
    levels = main // LANES
    block = LANES
    shape = (block, levels * block)
    r, c = iota(shape, 0), iota(shape, 1)
    pick = ((c % block) == (r // SLOTS) * SLOTS + SLOTS - 1) & ((c // block) == r % SLOTS)
    pick = pick.astype(jnp.bfloat16)
    full_ref[:, :main] = got_ref[...]
    for b in range(count // block):
        rows = got_ref[b * block : (b + 1) * block, :]
        stacked = jnp.concatenate([rows[:, j * LANES : (j + 1) * LANES] for j in range(levels)], axis=0)
        full_ref[b * block : (b + 1) * block, main:] = dot(pick, stacked).astype(jnp.bfloat16)


def key_bias(full_ref):
    count = full_ref.shape[0]
    first = (iota((SLOTS, LANES), 1) == 0).astype(jnp.bfloat16)
    lead = dot_t(first, full_ref[:, :LANES])[:1]
    level = iota((1, count), 1) % SLOTS
    return jnp.where((lead > 0.5 * ABSENT + 8.0) | (level == SLOTS - 1), HIDDEN, 0.0)


TILE = 128


def own_kernel(got_ref, full_ref, peak_ref, total_ref):
    full_rows(got_ref, full_ref)
    count, width = full_ref.shape
    scale = width ** -0.5
    bias = key_bias(full_ref)
    for t in range(count // TILE):
        q = full_ref[t * TILE : (t + 1) * TILE, :]
        scores = dot_t(q, full_ref[...]) * scale + bias
        me = iota(scores.shape, 1) == iota(scores.shape, 0) + t * TILE
        scores = jnp.where(me, HIDDEN, scores)
        peak = jnp.maximum(jnp.max(scores, axis=1, keepdims=True), prior_score)
        total = jnp.exp(prior_score - peak) + jnp.sum(jnp.exp(scores - peak), axis=1, keepdims=True)
        peak_ref[t * TILE : (t + 1) * TILE, :] = peak
        total_ref[t * TILE : (t + 1) * TILE, :] = total


def other_kernel(own_ref, got_ref, peak_ref, total_ref, density_ref, full_ref):
    full_rows(got_ref, full_ref)
    count, width = full_ref.shape
    scale = width ** -0.5
    bias = key_bias(full_ref)
    for t in range(count // TILE):
        q = own_ref[t * TILE : (t + 1) * TILE, :]
        scores = dot_t(q, full_ref[...]) * scale + bias
        before = peak_ref[t * TILE : (t + 1) * TILE, :]
        peak = jnp.maximum(jnp.max(scores, axis=1, keepdims=True), before)
        total = total_ref[t * TILE : (t + 1) * TILE, :] * jnp.exp(before - peak) + jnp.sum(
            jnp.exp(scores - peak), axis=1, keepdims=True
        )
        density = peak + jnp.log(total)
        spread = jnp.where(
            iota((TILE, LANES), 1) == iota((TILE, LANES), 0) % SLOTS, density, 0.0
        ).reshape(TILE // SLOTS, SLOTS, LANES)
        density_ref[t * TILE // SLOTS : (t + 1) * TILE // SLOTS] = jnp.sum(spread, axis=1, keepdims=True)


def pick_kernel(returned_ref, slot_ref, density_ref):
    owners = returned_ref.shape[0]
    values = returned_ref[...].reshape(owners, LANES)
    slot = slot_ref[...]
    count = slot.shape[1]
    named = (iota((owners, count), 0) == slot // SLOTS).astype(jnp.bfloat16)
    turned = values.T[:SLOTS]
    high = turned.astype(jnp.bfloat16)
    left = turned - high.astype(jnp.float32)
    middle = left.astype(jnp.bfloat16)
    low = (left - middle.astype(jnp.float32)).astype(jnp.bfloat16)
    picked = (dot(low, named) + dot(middle, named)) + dot(high, named)
    mine = iota((SLOTS, count), 0) == slot % SLOTS
    density_ref[...] = jnp.sum(jnp.where(mine, picked, 0.0), axis=0, keepdims=True)


def shards(embeddings, cluster):
    owners = lax.axis_size("gx")
    row_count, width = embeddings.shape
    main = width - LANES
    slot_count = owners * SLOTS
    send, slot = pack(cluster.reshape(1, row_count), embeddings)
    got = lax.all_to_all(
        send.reshape(owners, SLOTS, main), "gx", split_axis=0, concat_axis=0, tiled=True
    ).reshape(slot_count, main)
    other = lax.ppermute(got, "gy", [(0, 1), (1, 0)])
    own, peak, total = pl.pallas_call(
        own_kernel,
        out_shape=(
            jax.ShapeDtypeStruct((slot_count, width), jnp.bfloat16),
            jax.ShapeDtypeStruct((slot_count, 1), jnp.float32),
            jax.ShapeDtypeStruct((slot_count, 1), jnp.float32),
        ),
        name="own",
    )(got)
    density = pl.pallas_call(
        other_kernel,
        out_shape=jax.ShapeDtypeStruct((owners, 1, LANES), jnp.float32),
        scratch_shapes=[pltpu.VMEM((slot_count, width), jnp.bfloat16)],
        name="other",
    )(own, other, peak, total)
    returned = lax.all_to_all(density, "gx", split_axis=0, concat_axis=0, tiled=True)
    picked = pl.pallas_call(
        pick_kernel,
        out_shape=jax.ShapeDtypeStruct((1, row_count), jnp.float32),
        name="pick",
    )(returned, slot)
    return picked.reshape(row_count)


def solution(mesh):
    return jax.shard_map(
        shards,
        mesh=mesh,
        in_specs=(P(("gx", "gy"), None), P(("gx", "gy"), None)),
        out_specs=P(("gx", "gy")),
        check_vma=False,
    )
```

time: 138 us -> 108 us (0.78)
  Pallas kernels: 0 us -> 23.9 us
  local copies, waits for them, and re-layouts: 21 us -> 0.01 us
  waiting for transfers between devices: 13.6 us -> 0.01 us
  other arithmetic: 9.97 us -> 0 us
  matrix products: 9.14 us -> 0 us
  blocking collectives: 74.4 us -> 81.4 us
  starting transfers between devices: 9.09 us -> 2.47 us
    pallas_call x0 -> x4, Pallas kernels: none -> 23.9 us  [the longest x1 9.02 us: shards(): pl.pallas_call(other_kernel, out_shape=jax.ShapeDtypeStruct((owners, 1, L...]
    all_to_all x1 -> x0, waiting for transfers between devices: 10.6 us -> none  [shards(): lax.all_to_all(density_slots.reshape(owners, capacity), 'gx', split_axis=...]
    dot_general x1 -> x0, matrix products: 9.14 us -> none  [fold_block(): jnp.einsum('qd,kd->qk', own_rows, key_rows, preferred_element_type=jnp.fl...]
    scatter x2 -> x0, local copies, waits for them, and re-layouts: 7.76 us -> none  [the longest x1 4.4 us: shards(): jnp.zeros((slot_count, width), jnp.bfloat16).at[slot_index].set(embeddings)]
    all_to_all x1 -> x2, blocking collectives: 74.4 us -> 81.4 us  [the longest x1 63.6 us: shards(): lax.all_to_all(send.reshape(owners, SLOTS, main), 'gx', split_axis=0, con...]
    reshape x3 -> x0, local copies, waits for them, and re-layouts: 6.65 us -> none  [the longest x1 3.86 us: shards(): own_rows = recv_rows.reshape(slot_count, width)]
    reduce_sum x2 -> x0, other arithmetic: 6.2 us -> none  [the longest x1 5.28 us: fold_block(): jnp.sum(terms, axis=1)]
    all_to_all x1 -> x0, starting transfers between devices: 6.17 us -> none  [shards(): lax.all_to_all(density_slots.reshape(owners, capacity), 'gx', split_axis=...]
  transfers between devices with their start and end apart: 3 -> 1, of which waited for: 2 -> 0; matrix products, arithmetic and copies ran while one was open for 0% -> 0% of each run, Pallas kernels for 0% -> 8%
where the time goes in v1:
time: 108 us
  blocking collectives  81.4 us (75%)
  Pallas kernels  23.9 us (22%)
  starting transfers between devices  2.47 us (2%)
    all_to_all x1, blocking collectives, shards(): lax.all_to_all(send.reshape(owners, SLOTS, main), 'gx', split_axis=0, con...  63.6 us
    all_to_all x1, blocking collectives, shards(): lax.all_to_all(density, 'gx', split_axis=0, concat_axis=0, tiled=True)  17.8 us
    pallas_call x1, Pallas kernels, shards(): pl.pallas_call(other_kernel, out_shape=jax.ShapeDtypeStruct((owners, 1, L...  9.02 us
    pallas_call x1, Pallas kernels, shards(): pl.pallas_call(own_kernel, out_shape=(jax.ShapeDtypeStruct((slot_count, w...  8.19 us
    pallas_call x1, Pallas kernels, pack(): pl.pallas_call(pack_kernel, out_shape=(jax.ShapeDtypeStruct((owners * SLO...  5.06 us
    ppermute x1, starting transfers between devices, shards(): other = lax.ppermute(got, 'gy', [(0, 1), (1, 0)])  2.47 us
  transfers between devices with their start and end apart: 1, of which 0 were waited for; matrix products, arithmetic and copies ran while one was open for 0% of the time, Pallas kernels for 8%

profile of v1, /device:TPU:1, one launch (start us, length us, event | category | flops | bytes accessed | tf_op | source)
XLA Modules:
  0.0 107.8 jit_solution(8745657894702107548)
XLA Ops:
  0.0 5.1 %pack.1 = (bf16[1024,896]{1,0:T(8,128)(2,1)}, s32[1,448]{1,0:T(1,128)}) custom-call(s32[1,448]{1,0:T(1,128)} %bitcast.7, bf16[448,1024]{1,0:T(8,128)(2,1)} %rows_ref.1), custom_call_target="tpu_custom_call" | custom-call | tf_op jit(solution)/shard_map/pack/pallas_call | solution.py:67
  5.1 63.6 %all_to_all.10 = bf16[128,8,896]{2,1,0:T(8,128)(2,1)S(1)} all-to-all(bf16[128,8,896]{2,1,0:T(8,128)(2,1)} %bitcast.6), channel_id=1, replica_groups=mesh['gx'=128,'gy'=2] {'gx'}, dimensions={0} | all-to-all | bytes 3670016 | tf_op jit(solution)/shard_map/all_to_all | solution.py:161
  68.6 0.0 copy-start
  68.7 2.5 %collective-permute-start = (bf16[1024,896]{1,0:T(8,128)(2,1)S(1)}, bf16[1024,896]{1,0:T(8,128)(2,1)}, u32[]{:S(2)}, u32[]{:S(2)}) collective-permute-start(bf16[1024,896]{1,0:T(8,128)(2,1)S(1)} %bitcast.4), channel_id=1, source_target_pairs={{0,1},{1,0},{2,3},{3,2},{4,5},{5,4},{6,7},{7,6},{8,9},{9,8},{10,11... | collective-permute-start | bytes 5505032 | tf_op jit(solution)/shard_map/ppermute | solution.py:164
  71.1 0.0 copy-done
  71.1 8.2 %own.1 = (bf16[1024,1024]{1,0:T(8,128)(2,1)}, f32[1024,1]{1,0:T(8,128)}, f32[1024,1]{1,0:T(8,128)}) custom-call(bf16[1024,896]{1,0:T(8,128)(2,1)} %bitcast.5), custom_call_target="tpu_custom_call" | custom-call | tf_op jit(solution)/shard_map/own/pallas_call | solution.py:165
  79.3 0.0 collective-permute-done.got_ref
  79.3 9.0 %other.1 = f32[128,1,128]{2,1,0:T(1,128)} custom-call(bf16[1024,1024]{1,0:T(8,128)(2,1)} %get-tuple-element.11.own_ref, bf16[1024,896]{1,0:T(8,128)(2,1)} %collective-permute-done.got_ref, f32[1024,1]{1,0:T(8,128)} %get-tuple-element.12.peak_ref, f32[1024,1]{1,0:T(8,128)} %get-tuple-element.13.total_ref), custom_call_target="tpu_custom_call" | custom-call | tf_op jit(solution)/shard_map/other/pallas_call | solution.py:174
  88.3 17.8 %all_to_all.11.returned_ref = f32[128,1,128]{2,1,0:T(1,128)} all-to-all(f32[128,1,128]{2,1,0:T(1,128)} %other.1), channel_id=1, replica_groups=mesh['gx'=128,'gy'=2] {'gx'}, dimensions={0} | all-to-all | bytes 131072 | tf_op jit(solution)/shard_map/all_to_all | solution.py:180
  106.1 1.7 %pick.1 = f32[1,448]{1,0:T(1,128)} custom-call(f32[128,1,128]{2,1,0:T(1,128)} %all_to_all.11.returned_ref, s32[1,448]{1,0:T(1,128)} %get-tuple-element.14.slot_ref), custom_call_target="tpu_custom_call" | custom-call | tf_op jit(solution)/shard_map/pick/pallas_call | solution.py:181
Async XLA Ops:
  68.6 2.5 %copy-start = (bf16[128,8,896]{2,1,0:T(8,128)(2,1)}, bf16[128,8,896]{2,1,0:T(8,128)(2,1)S(1)}, u32[]{:S(2)}) copy-start(bf16[128,8,896]{2,1,0:T(8,128)(2,1)S(1)} %all_to_all.10) | copy-start | bytes 5505028
  68.7 10.7 %collective-permute-start = (bf16[1024,896]{1,0:T(8,128)(2,1)S(1)}, bf16[1024,896]{1,0:T(8,128)(2,1)}, u32[]{:S(2)}, u32[]{:S(2)}) collective-permute-start(bf16[1024,896]{1,0:T(8,128)(2,1)S(1)} %bitcast.4), channel_id=1, source_target_pairs={{0,1},{1,0},{2,3},{3,2},{4,5},{5,4},{6,7},{7,6},{8,9},{9,8},{10,11... | collective-permute-start | bytes 5505032 | tf_op jit(solution)/shard_map/ppermute | solution.py:164

commit v2 on v1

v2 whole, which is shorter than its diff:
```python
import math

import jax
import jax.numpy as jnp
from jax import lax
from jax.experimental import pallas as pl
from jax.experimental.pallas import tpu as pltpu
from jax.sharding import PartitionSpec as P

LOG2E = math.log2(math.e)
LN2 = math.log(2.0)
PRIOR = 6.0
ABSENT = 32.0
HIDDEN = -1e30
LANES = 128
SLOTS = 8
LAST = SLOTS - 1
ROWS = 512
TILE = 64


def iota(shape, dim):
    return lax.broadcasted_iota(jnp.int32, shape, dim)


def dot(a, b):
    return jnp.dot(a, b, preferred_element_type=jnp.float32)


def dot_t(a, b):
    return lax.dot_general(a, b, (((1,), (1,)), ((), ())), preferred_element_type=jnp.float32)


def on_chip(x):
    return pltpu.with_memory_space_constraint(x, pltpu.VMEM)


def chunk_of(j):
    return slice(j * LANES, (j + 1) * LANES)


VMEM_SPEC = pl.BlockSpec(memory_space=pltpu.VMEM)
ANY_SPEC = pl.BlockSpec(memory_space=pl.ANY)
PARAMS = pltpu.CompilerParams(vmem_limit_bytes=16 << 20)


def pack_kernel(cluster_ref, rows_hbm, send_ref, slot_ref, rows_ref, place_ref, sem):
    copy = pltpu.make_async_copy(rows_hbm, rows_ref, sem)
    copy.start()
    row_count, width = rows_ref.shape
    count, main = send_ref.shape
    owners = count // SLOTS
    ids = cluster_ref[...]
    named = iota((owners, row_count), 0) == ids
    before = (iota((row_count, row_count), 0) < iota((row_count, row_count), 1)).astype(jnp.bfloat16)
    earlier = dot(named.astype(jnp.bfloat16), before)
    rank = jnp.sum(jnp.where(named, earlier, 0.0), axis=0, keepdims=True).astype(jnp.int32)
    slot = ids * SLOTS + rank
    slot_ref[...] = slot
    place = (iota((count, row_count), 0) == slot).astype(jnp.float32)
    filled = jnp.sum(place, axis=1, keepdims=True)
    place_ref[...] = place.astype(jnp.bfloat16)
    copy.wait()
    level = iota((owners, SLOTS, LANES), 1)
    rest = None
    for n in reversed(range(width // (2 * LANES))):
        pair = dot(place_ref[...], rows_ref[:, 2 * n * LANES : 2 * (n + 1) * LANES])
        for j in (2 * n, 2 * n + 1):
            chunk = pair[:, (j % 2) * LANES : (j % 2 + 1) * LANES]
            if rest is None:
                rest = pair[:, LANES:].reshape(owners, SLOTS, LANES)
            if j * LANES == main:
                continue
            if j == 0:
                empty = (iota((count, LANES), 1) == 0) & (filled == 0.0)
                chunk = jnp.where(empty, ABSENT, chunk)
            moved = pltpu.roll(rest, (LAST - j) % SLOTS, 1)
            chunk = jnp.where(level == LAST, moved, chunk.reshape(owners, SLOTS, LANES))
            send_ref[:, chunk_of(j)] = chunk.reshape(count, LANES).astype(jnp.bfloat16)


def full_rows(got_ref, full_ref):
    count, main = got_ref.shape
    shape = (count // SLOTS, SLOTS, LANES)
    level = iota(shape, 1)
    full_ref[:, :main] = got_ref[...]
    rest = jnp.zeros(shape, jnp.float32)
    for j in range(main // LANES):
        chunk = got_ref[:, chunk_of(j)].astype(jnp.float32).reshape(shape)
        rest = jnp.where(level == j, pltpu.roll(chunk, (j - LAST) % SLOTS, 1), rest)
    full_ref[:, main:] = rest.reshape(count, LANES).astype(jnp.bfloat16)


def key_bias(full_ref):
    count = full_ref.shape[0]
    first = (iota((SLOTS, LANES), 1) == 0).astype(jnp.bfloat16)
    lead = dot_t(first, full_ref[:, :LANES])[:1]
    level = iota((1, count), 1) % SLOTS
    return jnp.where((lead > 0.75 * ABSENT) | (level == LAST), HIDDEN, 0.0)


def score_rows(query_ref, key_ref, bias, scores_ref, m, own):
    count, width = key_ref.shape
    wide = 2 * LANES
    first = m * ROWS
    for n in range(count // wide):
        scores = dot_t(query_ref[first : first + ROWS, :], key_ref[n * wide : (n + 1) * wide, :])
        scores = scores * (LOG2E * width**-0.5) + bias[:, n * wide : (n + 1) * wide]
        if own and first <= n * wide < first + ROWS:
            me = iota(scores.shape, 1) + (n * wide - first) == iota(scores.shape, 0)
            scores = jnp.where(me, HIDDEN, scores)
        scores_ref[first : first + ROWS, n * wide : (n + 1) * wide] = scores


def own_kernel(got_ref, full_ref, peak_ref, total_ref, scores_ref):
    full_rows(got_ref, full_ref)
    bias = key_bias(full_ref)
    for m in range(full_ref.shape[0] // ROWS):
        score_rows(full_ref, full_ref, bias, scores_ref, m, True)
        for t in range(m * ROWS, (m + 1) * ROWS, TILE):
            scores = scores_ref[t : t + TILE, :]
            peak = jnp.maximum(jnp.max(scores, axis=1, keepdims=True), PRIOR)
            total = jnp.exp2(PRIOR - peak) + jnp.sum(jnp.exp2(scores - peak), axis=1, keepdims=True)
            peak_ref[t : t + TILE, :] = peak
            total_ref[t : t + TILE, :] = total


def other_kernel(own_ref, got_ref, peak_ref, total_ref, density_ref, full_ref, scores_ref):
    full_rows(got_ref, full_ref)
    bias = key_bias(full_ref)
    for m in range(full_ref.shape[0] // ROWS):
        score_rows(own_ref, full_ref, bias, scores_ref, m, False)
        for t in range(m * ROWS, (m + 1) * ROWS, TILE):
            scores = scores_ref[t : t + TILE, :]
            before = peak_ref[t : t + TILE, :]
            peak = jnp.maximum(jnp.max(scores, axis=1, keepdims=True), before)
            total = total_ref[t : t + TILE, :] * jnp.exp2(before - peak) + jnp.sum(
                jnp.exp2(scores - peak), axis=1, keepdims=True
            )
            density = peak * LN2 + jnp.log(total)
            mine = iota((TILE, LANES), 1) == iota((TILE, LANES), 0) % SLOTS
            spread = jnp.where(mine, density, 0.0).reshape(TILE // SLOTS, SLOTS, LANES)
            density_ref[t // SLOTS : (t + TILE) // SLOTS] = jnp.sum(spread, axis=1, keepdims=True)


def pick_kernel(returned_ref, slot_ref, density_ref):
    owners = returned_ref.shape[0]
    values = returned_ref[...].reshape(owners, LANES)
    slot = slot_ref[...]
    count = slot.shape[1]
    named = (iota((owners, count), 0) == slot // SLOTS).astype(jnp.bfloat16)
    turned = values.T[:SLOTS]
    high = turned.astype(jnp.bfloat16)
    left = turned - high.astype(jnp.float32)
    middle = left.astype(jnp.bfloat16)
    low = (left - middle.astype(jnp.float32)).astype(jnp.bfloat16)
    picked = (dot(low, named) + dot(middle, named)) + dot(high, named)
    mine = iota((SLOTS, count), 0) == slot % SLOTS
    density_ref[...] = jnp.sum(jnp.where(mine, picked, 0.0), axis=0, keepdims=True)


def shards(embeddings, cluster):
    owners = lax.axis_size("gx")
    row_count, width = embeddings.shape
    main = width - LANES
    slot_count = owners * SLOTS
    send, slot = pl.pallas_call(
        pack_kernel,
        in_specs=[VMEM_SPEC, ANY_SPEC],
        out_shape=(
            jax.ShapeDtypeStruct((slot_count, main), jnp.bfloat16),
            pltpu.VMEM((1, row_count), jnp.int32),
        ),
        scratch_shapes=[
            pltpu.VMEM((row_count, width), jnp.bfloat16),
            pltpu.VMEM((slot_count, row_count), jnp.bfloat16),
            pltpu.SemaphoreType.DMA,
        ],
        compiler_params=PARAMS,
        name="pack",
    )(
        cluster.reshape(1, row_count),
        pltpu.with_memory_space_constraint(embeddings, pltpu.HBM),
    )
    got = lax.all_to_all(
        send.reshape(owners, SLOTS, main), "gx", split_axis=0, concat_axis=0, tiled=True
    ).reshape(slot_count, main)
    other = lax.ppermute(got, "gy", [(0, 1), (1, 0)])
    own, peak, total = pl.pallas_call(
        own_kernel,
        in_specs=[VMEM_SPEC],
        out_shape=(
            pltpu.VMEM((slot_count, width), jnp.bfloat16),
            pltpu.VMEM((slot_count, 1), jnp.float32),
            pltpu.VMEM((slot_count, 1), jnp.float32),
        ),
        scratch_shapes=[pltpu.VMEM((slot_count, slot_count), jnp.float32)],
        compiler_params=PARAMS,
        name="own",
    )(on_chip(got))
    density = pl.pallas_call(
        other_kernel,
        in_specs=[VMEM_SPEC] * 4,
        out_shape=jax.ShapeDtypeStruct((owners, 1, LANES), jnp.float32),
        scratch_shapes=[
            pltpu.VMEM((slot_count, width), jnp.bfloat16),
            pltpu.VMEM((slot_count, slot_count), jnp.float32),
        ],
        compiler_params=PARAMS,
        name="other",
    )(on_chip(own), on_chip(other), on_chip(peak), on_chip(total))
    returned = lax.all_to_all(density, "gx", split_axis=0, concat_axis=0, tiled=True)
    picked = pl.pallas_call(
        pick_kernel,
        in_specs=[VMEM_SPEC, VMEM_SPEC],
        out_shape=jax.ShapeDtypeStruct((1, row_count), jnp.float32),
        compiler_params=PARAMS,
        name="pick",
    )(on_chip(returned), on_chip(slot))
    return picked.reshape(row_count)


def solution(mesh):
    return jax.shard_map(
        shards,
        mesh=mesh,
        in_specs=(P(("gx", "gy"), None), P(("gx", "gy"), None)),
        out_specs=P(("gx", "gy")),
        check_vma=False,
    )
```

time: 108 us -> 93.8 us (0.87)
  Pallas kernels: 23.9 us -> 10.7 us
  blocking collectives: 81.4 us -> 79.5 us
    pallas_call x4, Pallas kernels: 23.9 us -> 10.7 us  [the longest x1 3.97 us: shards(): pl.pallas_call(other_kernel, in_specs=[VMEM_SPEC] * 4, out_shape=jax.Shap...]
    all_to_all x1, blocking collectives: 17.8 us -> 16.1 us  [shards(): lax.all_to_all(density, 'gx', split_axis=0, concat_axis=0, tiled=True)]
  transfers between devices with their start and end apart: 1 -> 1, of which waited for: 0 -> 1; matrix products, arithmetic and copies ran while one was open for 0% -> 0% of each run, Pallas kernels for 8% -> 3%
where the time goes in v2:
time: 93.8 us; the launch traced here: 93.5 us
  blocking collectives  79.5 us (85%)
  Pallas kernels  10.7 us (11%)
  starting transfers between devices  2.48 us (3%)
    all_to_all x1, blocking collectives, shards(): lax.all_to_all(send.reshape(owners, SLOTS, main), 'gx', split_axis=0, con...  63.4 us
    all_to_all x1, blocking collectives, shards(): lax.all_to_all(density, 'gx', split_axis=0, concat_axis=0, tiled=True)  16.1 us
    pallas_call x1, Pallas kernels, shards(): pl.pallas_call(other_kernel, in_specs=[VMEM_SPEC] * 4, out_shape=jax.Shap...  3.97 us
    pallas_call x1, Pallas kernels, shards(): pl.pallas_call(own_kernel, in_specs=[VMEM_SPEC], out_shape=(pltpu.VMEM((s...  3.19 us
    pallas_call x1, Pallas kernels, shards(): pl.pallas_call(pack_kernel, in_specs=[VMEM_SPEC, ANY_SPEC], out_shape=(ja...  2.69 us
    ppermute x1, starting transfers between devices, shards(): other = lax.ppermute(got, 'gy', [(0, 1), (1, 0)])  2.48 us
  transfers between devices with their start and end apart: 1, of which 1 were waited for; matrix products, arithmetic and copies ran while one was open for 0% of the time, Pallas kernels for 3%

profile of v2, /device:TPU:1, one launch (start us, length us, event | category | flops | bytes accessed | tf_op | source)
XLA Modules:
  0.0 93.5 jit_solution(6596064627230701464)
XLA Ops:
  0.0 0.0 copy-start
  0.0 0.7 copy-done
  0.7 2.7 %pack.1 = (bf16[1024,896]{1,0:T(8,128)(2,1)S(1)}, s32[1,448]{1,0:T(1,128)S(1)}) custom-call(s32[1,448]{1,0:T(1,128)S(1)} %bitcast.7, bf16[448,1024]{1,0:T(8,128)(2,1)} %rows_hbm.1), custom_call_target="tpu_custom_call" | custom-call | tf_op jit(solution)/shard_map/pack/pallas_call | solution.py:167
  3.4 63.4 %all_to_all.10 = bf16[128,8,896]{2,1,0:T(8,128)(2,1)S(1)} all-to-all(bf16[128,8,896]{2,1,0:T(8,128)(2,1)S(1)} %bitcast.6), channel_id=1, replica_groups=mesh['gx'=128,'gy'=2] {'gx'}, dimensions={0} | all-to-all | bytes 3670016 | tf_op jit(solution)/shard_map/all_to_all | solution.py:185
  66.8 2.5 %collective-permute-start = (bf16[1024,896]{1,0:T(8,128)(2,1)S(1)}, bf16[1024,896]{1,0:T(8,128)(2,1)S(1)}, u32[]{:S(2)}, u32[]{:S(2)}) collective-permute-start(bf16[1024,896]{1,0:T(8,128)(2,1)S(1)} %bitcast.4), channel_id=1, source_target_pairs={{0,1},{1,0},{2,3},{3,2},{4,5},{5,4},{6,7},{7,6},{8,9},{9,8},{10,11... | collective-permute-start | bytes 5505032 | tf_op jit(solution)/shard_map/ppermute | solution.py:188
  69.2 3.2 %own.1 = (bf16[1024,1024]{1,0:T(8,128)(2,1)S(1)}, f32[1024,1]{1,0:T(8,128)S(1)}, f32[1024,1]{1,0:T(8,128)S(1)}) custom-call(bf16[1024,896]{1,0:T(8,128)(2,1)S(1)} %bitcast.5), custom_call_target="tpu_custom_call" | custom-call | tf_op jit(solution)/shard_map/own/pallas_call | solution.py:189
  72.4 0.2 collective-permute-done.got_ref
  72.6 4.0 %other.1 = f32[128,1,128]{2,1,0:T(1,128)S(1)} custom-call(bf16[1024,1024]{1,0:T(8,128)(2,1)S(1)} %get-tuple-element.11.own_ref, bf16[1024,896]{1,0:T(8,128)(2,1)S(1)} %collective-permute-done.got_ref, f32[1024,1]{1,0:T(8,128)S(1)} %get-tuple-element.12.peak_ref, f32[1024,1]{1,0:T(8,128)S(1)} %get-tuple-element.13.total_ref), custom_call_target="tpu_custom_call" | custom-call | tf_op jit(solution)/shard_map/other/pallas_call | solution.py:201
  76.6 16.1 %all_to_all.11.returned_ref = f32[128,1,128]{2,1,0:T(1,128)S(1)} all-to-all(f32[128,1,128]{2,1,0:T(1,128)S(1)} %other.1), channel_id=1, replica_groups=mesh['gx'=128,'gy'=2] {'gx'}, dimensions={0} | all-to-all | bytes 131072 | tf_op jit(solution)/shard_map/all_to_all | solution.py:212
  92.7 0.8 pick.1
Async XLA Ops:
  0.0 0.7 copy-start
  66.8 5.9 %collective-permute-start = (bf16[1024,896]{1,0:T(8,128)(2,1)S(1)}, bf16[1024,896]{1,0:T(8,128)(2,1)S(1)}, u32[]{:S(2)}, u32[]{:S(2)}) collective-permute-start(bf16[1024,896]{1,0:T(8,128)(2,1)S(1)} %bitcast.4), channel_id=1, source_target_pairs={{0,1},{1,0},{2,3},{3,2},{4,5},{5,4},{6,7},{7,6},{8,9},{9,8},{10,11... | collective-permute-start | bytes 5505032 | tf_op jit(solution)/shard_map/ppermute | solution.py:188

commit v3 on v2

v3 whole, which is shorter than its diff:
```python
import math

import jax
import jax.numpy as jnp
from jax import lax
from jax.experimental import pallas as pl
from jax.experimental.pallas import tpu as pltpu
from jax.sharding import PartitionSpec as P

LOG2E = math.log2(math.e)
LN2 = math.log(2.0)
PRIOR = 6.0
ABSENT = 32.0
HIDDEN = -1e30
LANES = 128
SLOTS = 8
LAST = SLOTS - 1
SHARED = LANES // SLOTS
BLOCK = 512
PART = 512
COPIES = 4


def iota(shape, dim):
    return lax.broadcasted_iota(jnp.int32, shape, dim)


def dot(a, b):
    return jnp.dot(a, b, preferred_element_type=jnp.float32)


def dot_t(a, b):
    return lax.dot_general(a, b, (((1,), (1,)), ((), ())), preferred_element_type=jnp.float32)


def on_chip(x):
    return pltpu.with_memory_space_constraint(x, pltpu.VMEM)


def chunk_of(j):
    return slice(j * LANES, (j + 1) * LANES)


VMEM_SPEC = pl.BlockSpec(memory_space=pltpu.VMEM)
ANY_SPEC = pl.BlockSpec(memory_space=pl.ANY)
PARAMS = pltpu.CompilerParams(vmem_limit_bytes=16 << 20)


def pack_kernel(cluster_hbm, rows_hbm, send_ref, slot_ref, cluster_ref, rows_ref, place_ref, sems):
    row_count, width = rows_ref.shape
    part = row_count // COPIES
    ids_copy = pltpu.make_async_copy(cluster_hbm, cluster_ref, sems.at[COPIES])
    ids_copy.start()
    copies = []
    for n in range(COPIES):
        some = slice(n * part, (n + 1) * part)
        copies.append(pltpu.make_async_copy(rows_hbm.at[some, :], rows_ref.at[some, :], sems.at[n]))
        copies[n].start()
    count, main = send_ref.shape
    owners = count // SLOTS
    before = (iota((row_count, row_count), 0) < iota((row_count, row_count), 1)).astype(jnp.bfloat16)
    ids_copy.wait()
    ids = cluster_ref[...]
    named = iota((owners, row_count), 0) == ids
    earlier = dot(named.astype(jnp.bfloat16), before)
    rank = jnp.sum(jnp.where(named, earlier, 0.0), axis=0, keepdims=True).astype(jnp.int32)
    slot = ids * SLOTS + rank
    slot_ref[...] = slot
    place = (iota((count, row_count), 0) == slot).astype(jnp.float32)
    filled = jnp.sum(place, axis=1, keepdims=True)
    place_ref[...] = place.astype(jnp.bfloat16)
    level = iota((owners, SLOTS, LANES), 1)
    rest = None
    for copy in copies:
        copy.wait()
    for n in reversed(range(width // (2 * LANES))):
        pair = dot(place_ref[...], rows_ref[:, 2 * n * LANES : 2 * (n + 1) * LANES])
        for j in (2 * n, 2 * n + 1):
            chunk = pair[:, (j % 2) * LANES : (j % 2 + 1) * LANES]
            if rest is None:
                rest = pair[:, LANES:].reshape(owners, SLOTS, LANES)
            if j * LANES == main:
                continue
            if j == 0:
                empty = (iota((count, LANES), 1) == 0) & (filled == 0.0)
                chunk = jnp.where(empty, ABSENT, chunk)
            moved = pltpu.roll(rest, (LAST - j) % SLOTS, 1)
            chunk = jnp.where(level == LAST, moved, chunk.reshape(owners, SLOTS, LANES))
            send_ref[:, chunk_of(j)] = chunk.reshape(count, LANES).astype(jnp.bfloat16)


def full_rows(got_ref, full_ref):
    count, main = got_ref.shape
    shape = (count // SLOTS, SLOTS, LANES)
    level = iota(shape, 1)
    full_ref[:, :main] = got_ref[...]
    rest = jnp.zeros(shape, jnp.float32)
    for j in range(main // LANES):
        chunk = got_ref[:, chunk_of(j)].astype(jnp.float32).reshape(shape)
        rest = jnp.where(level == j, pltpu.roll(chunk, (j - LAST) % SLOTS, 1), rest)
    full_ref[:, main:] = rest.reshape(count, LANES).astype(jnp.bfloat16)


def hide_keys(full_ref, bias_ref):
    count = full_ref.shape[0]
    lead = full_ref[:, :LANES].astype(jnp.float32)[:, :1]
    level = iota((count, LANES), 0) % SLOTS
    bias_ref[...] = jnp.where((lead > 0.75 * ABSENT) | (level == LAST), HIDDEN, 0.0)


def score_part(key_ref, query_ref, bias_ref, scores_ref, n, part, own):
    width = key_ref.shape[1]
    keys = slice(part * PART, (part + 1) * PART)
    scores = dot_t(key_ref[keys, :], query_ref[n * BLOCK : (n + 1) * BLOCK, :])
    bias = jnp.concatenate([bias_ref[keys, :]] * (BLOCK // LANES), axis=1)
    scores = scores * (LOG2E * width**-0.5) + bias
    if own and part * PART <= n * BLOCK < (part + 1) * PART:
        me = iota(scores.shape, 0) == iota(scores.shape, 1) + (n * BLOCK - part * PART)
        scores = jnp.where(me, HIDDEN, scores)
    scores_ref[n, keys, :] = scores
    return jnp.max(scores, axis=0, keepdims=True)


def fold(key_ref, query_ref, bias_ref, scores_ref, own, before, finish):
    count = key_ref.shape[0]
    blocks, parts = count // BLOCK, count // PART
    peaks, totals = {}, {}
    for n in range(blocks + 1):
        if n < blocks:
            peaks[n], totals[n] = before(n)
            old, new = peaks[n], peaks[n]
        for part in range(parts):
            if n < blocks:
                new = jnp.maximum(
                    new, score_part(key_ref, query_ref, bias_ref, scores_ref, n, part, own)
                )
            if n > 0:
                scores = scores_ref[n - 1, part * PART : (part + 1) * PART, :]
                totals[n - 1] += jnp.sum(jnp.exp2(scores - peaks[n - 1]), axis=0, keepdims=True)
        if n < blocks:
            totals[n] = totals[n] * jnp.exp2(old - new)
            peaks[n] = new
        if n > 0:
            finish(n - 1, peaks[n - 1], totals[n - 1])


def own_kernel(got_ref, full_ref, peak_ref, total_ref, bias_ref, scores_ref):
    full_rows(got_ref, full_ref)
    hide_keys(full_ref, bias_ref)

    def before(n):
        return jnp.full((1, BLOCK), PRIOR, jnp.float32), jnp.ones((1, BLOCK), jnp.float32)

    def finish(n, peak, total):
        peak_ref[:, n * BLOCK : (n + 1) * BLOCK] = peak
        total_ref[:, n * BLOCK : (n + 1) * BLOCK] = total

    fold(full_ref, full_ref, bias_ref, scores_ref, True, before, finish)


def other_kernel(own_ref, got_ref, peak_ref, total_ref, density_ref, full_ref, bias_ref, scores_ref):
    full_rows(got_ref, full_ref)
    hide_keys(full_ref, bias_ref)

    def before(n):
        lanes = slice(n * BLOCK, (n + 1) * BLOCK)
        return peak_ref[:, lanes], total_ref[:, lanes]

    def finish(n, peak, total):
        density = peak * LN2 + jnp.log(total)
        for v in range(BLOCK // LANES):
            row = density[:, chunk_of(v)].reshape(1, 1, LANES)
            first = (n * BLOCK + v * LANES) // SLOTS
            density_ref[first : first + SHARED] = jnp.broadcast_to(row, (SHARED, 1, LANES))

    fold(full_ref, own_ref, bias_ref, scores_ref, False, before, finish)


def pick_kernel(returned_ref, slot_ref, density_ref):
    owners = returned_ref.shape[0]
    values = returned_ref[...].reshape(owners, LANES)
    slot = slot_ref[...]
    count = slot.shape[1]
    named = (iota((owners, count), 0) == slot // SLOTS).astype(jnp.bfloat16)
    turned = values.T
    high = turned.astype(jnp.bfloat16)
    left = turned - high.astype(jnp.float32)
    middle = left.astype(jnp.bfloat16)
    low = (left - middle.astype(jnp.float32)).astype(jnp.bfloat16)
    picked = (dot(low, named) + dot(middle, named)) + dot(high, named)
    lane = slot % SLOTS + (lax.axis_index("gx") % SHARED) * SLOTS
    mine = iota((LANES, count), 0) == lane
    density_ref[...] = jnp.sum(jnp.where(mine, picked, 0.0), axis=0, keepdims=True)


def shards(embeddings, cluster):
    owners = lax.axis_size("gx")
    row_count, width = embeddings.shape
    main = width - LANES
    slot_count = owners * SLOTS
    send, slot = pl.pallas_call(
        pack_kernel,
        in_specs=[ANY_SPEC, ANY_SPEC],
        out_shape=(
            jax.ShapeDtypeStruct((slot_count, main), jnp.bfloat16),
            pltpu.VMEM((1, row_count), jnp.int32),
        ),
        scratch_shapes=[
            pltpu.VMEM((1, row_count), jnp.int32),
            pltpu.VMEM((row_count, width), jnp.bfloat16),
            pltpu.VMEM((slot_count, row_count), jnp.bfloat16),
            pltpu.SemaphoreType.DMA((COPIES + 1,)),
        ],
        compiler_params=PARAMS,
        name="pack",
    )(
        pltpu.with_memory_space_constraint(cluster.reshape(1, row_count), pltpu.HBM),
        pltpu.with_memory_space_constraint(embeddings, pltpu.HBM),
    )
    got = lax.all_to_all(
        send.reshape(owners, SLOTS, main), "gx", split_axis=0, concat_axis=0, tiled=True
    ).reshape(slot_count, main)
    other = lax.ppermute(got, "gy", [(0, 1), (1, 0)])
    own, peak, total = pl.pallas_call(
        own_kernel,
        in_specs=[VMEM_SPEC],
        out_shape=(
            pltpu.VMEM((slot_count, width), jnp.bfloat16),
            pltpu.VMEM((1, slot_count), jnp.float32),
            pltpu.VMEM((1, slot_count), jnp.float32),
        ),
        scratch_shapes=[
            pltpu.VMEM((slot_count, LANES), jnp.float32),
            pltpu.VMEM((slot_count // BLOCK, slot_count, BLOCK), jnp.float32),
        ],
        compiler_params=PARAMS,
        name="own",
    )(on_chip(got))
    density = pl.pallas_call(
        other_kernel,
        in_specs=[VMEM_SPEC] * 4,
        out_shape=jax.ShapeDtypeStruct((owners, 1, LANES), jnp.float32),
        scratch_shapes=[
            pltpu.VMEM((slot_count, width), jnp.bfloat16),
            pltpu.VMEM((slot_count, LANES), jnp.float32),
            pltpu.VMEM((slot_count // BLOCK, slot_count, BLOCK), jnp.float32),
        ],
        compiler_params=PARAMS,
        name="other",
    )(on_chip(own), on_chip(other), on_chip(peak), on_chip(total))
    returned = lax.all_to_all(density, "gx", split_axis=0, concat_axis=0, tiled=True)
    picked = pl.pallas_call(
        pick_kernel,
        in_specs=[VMEM_SPEC, VMEM_SPEC],
        out_shape=jax.ShapeDtypeStruct((1, row_count), jnp.float32),
        compiler_params=PARAMS,
        name="pick",
    )(on_chip(returned), on_chip(slot))
    return picked.reshape(row_count)


def solution(mesh):
    return jax.shard_map(
        shards,
        mesh=mesh,
        in_specs=(P(("gx", "gy"), None), P(("gx", "gy"), None)),
        out_specs=P(("gx", "gy")),
        check_vma=False,
    )
```

time: 93.8 us -> 92.3 us (0.984)
  Pallas kernels: 10.7 us -> 9.75 us
where the time goes in v3:
time: 92.3 us; the launch traced here: 92.1 us
  blocking collectives  79.5 us (86%)
  Pallas kernels  9.75 us (11%)
  starting transfers between devices  2.47 us (3%)
    all_to_all x1, blocking collectives, shards(): lax.all_to_all(send.reshape(owners, SLOTS, main), 'gx', split_axis=0, con...  63.4 us
    all_to_all x1, blocking collectives, shards(): lax.all_to_all(density, 'gx', split_axis=0, concat_axis=0, tiled=True)  16.1 us
    pallas_call x1, Pallas kernels, shards(): pl.pallas_call(other_kernel, in_specs=[VMEM_SPEC] * 4, out_shape=jax.Shap...  3.21 us
    pallas_call x1, Pallas kernels, shards(): pl.pallas_call(own_kernel, in_specs=[VMEM_SPEC], out_shape=(pltpu.VMEM((s...  3.05 us
    pallas_call x1, Pallas kernels, shards(): pl.pallas_call(pack_kernel, in_specs=[ANY_SPEC, ANY_SPEC], out_shape=(jax...  2.58 us
    ppermute x1, starting transfers between devices, shards(): other = lax.ppermute(got, 'gy', [(0, 1), (1, 0)])  2.47 us
  transfers between devices with their start and end apart: 1, of which 1 were waited for; matrix products, arithmetic and copies ran while one was open for 0% of the time, Pallas kernels for 3%

profile of v3, /device:TPU:1, one launch (start us, length us, event | category | flops | bytes accessed | tf_op | source)
XLA Modules:
  0.0 92.1 jit_solution(8414664071395073201)
XLA Ops:
  0.0 2.6 %pack.1 = (bf16[1024,896]{1,0:T(8,128)(2,1)S(1)}, s32[1,448]{1,0:T(1,128)S(1)}) custom-call(s32[1,448]{1,0:T(1,128)} %bitcast.7, bf16[448,1024]{1,0:T(8,128)(2,1)} %rows_hbm.1), custom_call_target="tpu_custom_call" | custom-call | tf_op jit(solution)/shard_map/pack/pallas_call | solution.py:201
  2.6 63.4 %all_to_all.10 = bf16[128,8,896]{2,1,0:T(8,128)(2,1)S(1)} all-to-all(bf16[128,8,896]{2,1,0:T(8,128)(2,1)S(1)} %bitcast.6), channel_id=1, replica_groups=mesh['gx'=128,'gy'=2] {'gx'}, dimensions={0} | all-to-all | bytes 3670016 | tf_op jit(solution)/shard_map/all_to_all | solution.py:220
  66.0 2.5 %collective-permute-start = (bf16[1024,896]{1,0:T(8,128)(2,1)S(1)}, bf16[1024,896]{1,0:T(8,128)(2,1)S(1)}, u32[]{:S(2)}, u32[]{:S(2)}) collective-permute-start(bf16[1024,896]{1,0:T(8,128)(2,1)S(1)} %bitcast.4), channel_id=1, source_target_pairs={{0,1},{1,0},{2,3},{3,2},{4,5},{5,4},{6,7},{7,6},{8,9},{9,8},{10,11... | collective-permute-start | bytes 5505032 | tf_op jit(solution)/shard_map/ppermute | solution.py:223
  68.5 3.1 %own.1 = (bf16[1024,1024]{1,0:T(8,128)(2,1)S(1)}, f32[1,1024]{1,0:T(1,128)S(1)}, f32[1,1024]{1,0:T(1,128)S(1)}) custom-call(bf16[1024,896]{1,0:T(8,128)(2,1)S(1)} %bitcast.5), custom_call_target="tpu_custom_call" | custom-call | tf_op jit(solution)/shard_map/own/pallas_call | solution.py:224
  71.5 0.4 collective-permute-done.got_ref
  71.9 3.2 %other.1 = f32[128,1,128]{2,1,0:T(1,128)S(1)} custom-call(bf16[1024,1024]{1,0:T(8,128)(2,1)S(1)} %get-tuple-element.11.own_ref, bf16[1024,896]{1,0:T(8,128)(2,1)S(1)} %collective-permute-done.got_ref, f32[1,1024]{1,0:T(1,128)S(1)} %get-tuple-element.12.peak_ref, f32[1,1024]{1,0:T(1,128)S(1)} %get-tuple-element.13.total_ref), custom_call_target="tpu_custom_call" | custom-call | tf_op jit(solution)/shard_map/other/pallas_call | solution.py:239
  75.1 16.1 %all_to_all.11.returned_ref = f32[128,1,128]{2,1,0:T(1,128)S(1)} all-to-all(f32[128,1,128]{2,1,0:T(1,128)S(1)} %other.1), channel_id=1, replica_groups=mesh['gx'=128,'gy'=2] {'gx'}, dimensions={0} | all-to-all | bytes 131072 | tf_op jit(solution)/shard_map/all_to_all | solution.py:251
  91.2 0.9 pick.1
Async XLA Ops:
  66.0 5.9 %collective-permute-start = (bf16[1024,896]{1,0:T(8,128)(2,1)S(1)}, bf16[1024,896]{1,0:T(8,128)(2,1)S(1)}, u32[]{:S(2)}, u32[]{:S(2)}) collective-permute-start(bf16[1024,896]{1,0:T(8,128)(2,1)S(1)} %bitcast.4), channel_id=1, source_target_pairs={{0,1},{1,0},{2,3},{3,2},{4,5},{5,4},{6,7},{7,6},{8,9},{9,8},{10,11... | collective-permute-start | bytes 5505032 | tf_op jit(solution)/shard_map/ppermute | solution.py:223

commit v4 on v3

--- a/solution.py
+++ b/solution.py
@@ -66,9 +66,15 @@
     rank = jnp.sum(jnp.where(named, earlier, 0.0), axis=0, keepdims=True).astype(jnp.int32)
     slot = ids * SLOTS + rank
     slot_ref[...] = slot
-    place = (iota((count, row_count), 0) == slot).astype(jnp.float32)
-    filled = jnp.sum(place, axis=1, keepdims=True)
-    place_ref[...] = place.astype(jnp.bfloat16)
+    some = 2 * SLOTS
+    ahead = jnp.broadcast_to(slot, (some, row_count)) - iota((some, row_count), 0)
+    ahead = ahead.astype(jnp.int16)
+    for i in range(count // some):
+        place_ref[i * some : (i + 1) * some, :] = jnp.where(
+            ahead == i * some, jnp.ones((), jnp.bfloat16), jnp.zeros((), jnp.bfloat16)
+        )
+    members = jnp.sum(named.astype(jnp.float32), axis=1, keepdims=True)
+    members = jnp.broadcast_to(members, (owners, LANES))[:, None, :]
     level = iota((owners, SLOTS, LANES), 1)
     rest = None
     for copy in copies:
@@ -81,11 +87,11 @@
                 rest = pair[:, LANES:].reshape(owners, SLOTS, LANES)
             if j * LANES == main:
                 continue
+            chunk = chunk.reshape(level.shape)
             if j == 0:
-                empty = (iota((count, LANES), 1) == 0) & (filled == 0.0)
-                chunk = jnp.where(empty, ABSENT, chunk)
-            moved = pltpu.roll(rest, (LAST - j) % SLOTS, 1)
-            chunk = jnp.where(level == LAST, moved, chunk.reshape(owners, SLOTS, LANES))
+                empty = level.astype(jnp.float32) >= jnp.broadcast_to(members, level.shape)
+                chunk = jnp.where(empty & (iota(level.shape, 2) == 0), ABSENT, chunk)
+            chunk = jnp.where(level == LAST, pltpu.roll(rest, (LAST - j) % SLOTS, 1), chunk)
             send_ref[:, chunk_of(j)] = chunk.reshape(count, LANES).astype(jnp.bfloat16)
 
 
@@ -182,14 +188,14 @@
     slot = slot_ref[...]
     count = slot.shape[1]
     named = (iota((owners, count), 0) == slot // SLOTS).astype(jnp.bfloat16)
-    turned = values.T
+    turn = (SHARED - lax.axis_index("gx") % SHARED) % SHARED * SLOTS
+    turned = pltpu.roll(values, turn, 1).T[:SLOTS]
     high = turned.astype(jnp.bfloat16)
     left = turned - high.astype(jnp.float32)
     middle = left.astype(jnp.bfloat16)
     low = (left - middle.astype(jnp.float32)).astype(jnp.bfloat16)
     picked = (dot(low, named) + dot(middle, named)) + dot(high, named)
-    lane = slot % SLOTS + (lax.axis_index("gx") % SHARED) * SLOTS
-    mine = iota((LANES, count), 0) == lane
+    mine = iota((SLOTS, count), 0) == slot % SLOTS
     density_ref[...] = jnp.sum(jnp.where(mine, picked, 0.0), axis=0, keepdims=True)
 
 

time: 92.3 us -> 92.3 us (level)
  no operation moved by 1% of the time
where the time goes in v4:
time: 92.3 us; the launch traced here: 92.1 us
  blocking collectives  79.5 us (86%)
  Pallas kernels  9.79 us (11%)
  starting transfers between devices  2.47 us (3%)
    all_to_all x1, blocking collectives, shards(): lax.all_to_all(send.reshape(owners, SLOTS, main), 'gx', split_axis=0, con...  63.4 us
    all_to_all x1, blocking collectives, shards(): lax.all_to_all(density, 'gx', split_axis=0, concat_axis=0, tiled=True)  16.1 us
    pallas_call x1, Pallas kernels, shards(): pl.pallas_call(other_kernel, in_specs=[VMEM_SPEC] * 4, out_shape=jax.Shap...  3.2 us
    pallas_call x1, Pallas kernels, shards(): pl.pallas_call(own_kernel, in_specs=[VMEM_SPEC], out_shape=(pltpu.VMEM((s...  3.09 us
    pallas_call x1, Pallas kernels, shards(): pl.pallas_call(pack_kernel, in_specs=[ANY_SPEC, ANY_SPEC], out_shape=(jax...  2.59 us
    ppermute x1, starting transfers between devices, shards(): other = lax.ppermute(got, 'gy', [(0, 1), (1, 0)])  2.47 us
  transfers between devices with their start and end apart: 1, of which 1 were waited for; matrix products, arithmetic and copies ran while one was open for 0% of the time, Pallas kernels for 3%

profile of v4, /device:TPU:1, one launch (start us, length us, event | category | flops | bytes accessed | tf_op | source)
XLA Modules:
  0.0 92.1 jit_solution(1796156509683851060)
XLA Ops:
  0.0 2.6 %pack.1 = (bf16[1024,896]{1,0:T(8,128)(2,1)S(1)}, s32[1,448]{1,0:T(1,128)S(1)}) custom-call(s32[1,448]{1,0:T(1,128)} %bitcast.7, bf16[448,1024]{1,0:T(8,128)(2,1)} %rows_hbm.1), custom_call_target="tpu_custom_call" | custom-call | tf_op jit(solution)/shard_map/pack/pallas_call | solution.py:207
  2.6 63.4 %all_to_all.10 = bf16[128,8,896]{2,1,0:T(8,128)(2,1)S(1)} all-to-all(bf16[128,8,896]{2,1,0:T(8,128)(2,1)S(1)} %bitcast.6), channel_id=1, replica_groups=mesh['gx'=128,'gy'=2] {'gx'}, dimensions={0} | all-to-all | bytes 3670016 | tf_op jit(solution)/shard_map/all_to_all | solution.py:226
  66.0 2.5 %collective-permute-start = (bf16[1024,896]{1,0:T(8,128)(2,1)S(1)}, bf16[1024,896]{1,0:T(8,128)(2,1)S(1)}, u32[]{:S(2)}, u32[]{:S(2)}) collective-permute-start(bf16[1024,896]{1,0:T(8,128)(2,1)S(1)} %bitcast.4), channel_id=1, source_target_pairs={{0,1},{1,0},{2,3},{3,2},{4,5},{5,4},{6,7},{7,6},{8,9},{9,8},{10,11... | collective-permute-start | bytes 5505032 | tf_op jit(solution)/shard_map/ppermute | solution.py:229
  68.5 3.1 %own.1 = (bf16[1024,1024]{1,0:T(8,128)(2,1)S(1)}, f32[1,1024]{1,0:T(1,128)S(1)}, f32[1,1024]{1,0:T(1,128)S(1)}) custom-call(bf16[1024,896]{1,0:T(8,128)(2,1)S(1)} %bitcast.5), custom_call_target="tpu_custom_call" | custom-call | tf_op jit(solution)/shard_map/own/pallas_call | solution.py:230
  71.6 0.3 collective-permute-done.got_ref
  71.9 3.2 %other.1 = f32[128,1,128]{2,1,0:T(1,128)S(1)} custom-call(bf16[1024,1024]{1,0:T(8,128)(2,1)S(1)} %get-tuple-element.11.own_ref, bf16[1024,896]{1,0:T(8,128)(2,1)S(1)} %collective-permute-done.got_ref, f32[1,1024]{1,0:T(1,128)S(1)} %get-tuple-element.12.peak_ref, f32[1,1024]{1,0:T(1,128)S(1)} %get-tuple-element.13.total_ref), custom_call_target="tpu_custom_call" | custom-call | tf_op jit(solution)/shard_map/other/pallas_call | solution.py:245
  75.1 16.1 %all_to_all.11.returned_ref = f32[128,1,128]{2,1,0:T(1,128)S(1)} all-to-all(f32[128,1,128]{2,1,0:T(1,128)S(1)} %other.1), channel_id=1, replica_groups=mesh['gx'=128,'gy'=2] {'gx'}, dimensions={0} | all-to-all | bytes 131072 | tf_op jit(solution)/shard_map/all_to_all | solution.py:257
  91.2 0.9 pick.1
Async XLA Ops:
  66.0 5.9 %collective-permute-start = (bf16[1024,896]{1,0:T(8,128)(2,1)S(1)}, bf16[1024,896]{1,0:T(8,128)(2,1)S(1)}, u32[]{:S(2)}, u32[]{:S(2)}) collective-permute-start(bf16[1024,896]{1,0:T(8,128)(2,1)S(1)} %bitcast.4), channel_id=1, source_target_pairs={{0,1},{1,0},{2,3},{3,2},{4,5},{5,4},{6,7},{7,6},{8,9},{9,8},{10,11... | collective-permute-start | bytes 5505032 | tf_op jit(solution)/shard_map/ppermute | solution.py:229

commit v5 on v4

--- a/solution.py
+++ b/solution.py
@@ -18,7 +18,7 @@
 SHARED = LANES // SLOTS
 BLOCK = 512
 PART = 512
-COPIES = 4
+COPIES = 1
 
 
 def iota(shape, dim):
@@ -117,7 +117,11 @@
 def score_part(key_ref, query_ref, bias_ref, scores_ref, n, part, own):
     width = key_ref.shape[1]
     keys = slice(part * PART, (part + 1) * PART)
-    scores = dot_t(key_ref[keys, :], query_ref[n * BLOCK : (n + 1) * BLOCK, :])
+    lanes = slice(n * BLOCK, (n + 1) * BLOCK)
+    if own:
+        scores = dot_t(key_ref[keys, :], query_ref[lanes, :])
+    else:
+        scores = dot(key_ref[keys, :], query_ref[:, lanes])
     bias = jnp.concatenate([bias_ref[keys, :]] * (BLOCK // LANES), axis=1)
     scores = scores * (LOG2E * width**-0.5) + bias
     if own and part * PART <= n * BLOCK < (part + 1) * PART:
@@ -150,7 +154,7 @@
             finish(n - 1, peaks[n - 1], totals[n - 1])
 
 
-def own_kernel(got_ref, full_ref, peak_ref, total_ref, bias_ref, scores_ref):
+def own_kernel(got_ref, turned_ref, peak_ref, total_ref, full_ref, bias_ref, scores_ref):
     full_rows(got_ref, full_ref)
     hide_keys(full_ref, bias_ref)
 
@@ -162,6 +166,7 @@
         total_ref[:, n * BLOCK : (n + 1) * BLOCK] = total
 
     fold(full_ref, full_ref, bias_ref, scores_ref, True, before, finish)
+    turned_ref[...] = full_ref[...].T
 
 
 def other_kernel(own_ref, got_ref, peak_ref, total_ref, density_ref, full_ref, bias_ref, scores_ref):
@@ -231,11 +236,12 @@
         own_kernel,
         in_specs=[VMEM_SPEC],
         out_shape=(
-            pltpu.VMEM((slot_count, width), jnp.bfloat16),
+            pltpu.VMEM((width, slot_count), jnp.bfloat16),
             pltpu.VMEM((1, slot_count), jnp.float32),
             pltpu.VMEM((1, slot_count), jnp.float32),
         ),
         scratch_shapes=[
+            pltpu.VMEM((slot_count, width), jnp.bfloat16),
             pltpu.VMEM((slot_count, LANES), jnp.float32),
             pltpu.VMEM((slot_count // BLOCK, slot_count, BLOCK), jnp.float32),
         ],

time: 92.3 us -> 92.1 us (level)
  no operation moved by 1% of the time
where the time goes in v5:
time: 92.1 us; the launch traced here: 92 us
  blocking collectives  79.5 us (86%)
  Pallas kernels  9.69 us (11%)
  starting transfers between devices  2.47 us (3%)
    all_to_all x1, blocking collectives, shards(): lax.all_to_all(send.reshape(owners, SLOTS, main), 'gx', split_axis=0, con...  63.4 us
    all_to_all x1, blocking collectives, shards(): lax.all_to_all(density, 'gx', split_axis=0, concat_axis=0, tiled=True)  16.1 us
    pallas_call x1, Pallas kernels, shards(): pl.pallas_call(other_kernel, in_specs=[VMEM_SPEC] * 4, out_shape=jax.Shap...  3.17 us
    pallas_call x1, Pallas kernels, shards(): pl.pallas_call(own_kernel, in_specs=[VMEM_SPEC], out_shape=(pltpu.VMEM((w...  3.14 us
    pallas_call x1, Pallas kernels, shards(): pl.pallas_call(pack_kernel, in_specs=[ANY_SPEC, ANY_SPEC], out_shape=(jax...  2.48 us
    ppermute x1, starting transfers between devices, shards(): other = lax.ppermute(got, 'gy', [(0, 1), (1, 0)])  2.47 us
  transfers between devices with their start and end apart: 1, of which 1 were waited for; matrix products, arithmetic and copies ran while one was open for 0% of the time, Pallas kernels for 3%

profile of v5, /device:TPU:1, one launch (start us, length us, event | category | flops | bytes accessed | tf_op | source)
XLA Modules:
  0.0 92.0 jit_solution(18040048494298891532)
XLA Ops:
  0.0 2.5 %pack.1 = (bf16[1024,896]{1,0:T(8,128)(2,1)S(1)}, s32[1,448]{1,0:T(1,128)S(1)}) custom-call(s32[1,448]{1,0:T(1,128)} %bitcast.7, bf16[448,1024]{1,0:T(8,128)(2,1)} %rows_hbm.1), custom_call_target="tpu_custom_call" | custom-call | tf_op jit(solution)/shard_map/pack/pallas_call | solution.py:212
  2.5 63.4 %all_to_all.10 = bf16[128,8,896]{2,1,0:T(8,128)(2,1)S(1)} all-to-all(bf16[128,8,896]{2,1,0:T(8,128)(2,1)S(1)} %bitcast.6), channel_id=1, replica_groups=mesh['gx'=128,'gy'=2] {'gx'}, dimensions={0} | all-to-all | bytes 3670016 | tf_op jit(solution)/shard_map/all_to_all | solution.py:231
  65.9 2.5 %collective-permute-start = (bf16[1024,896]{1,0:T(8,128)(2,1)S(1)}, bf16[1024,896]{1,0:T(8,128)(2,1)S(1)}, u32[]{:S(2)}, u32[]{:S(2)}) collective-permute-start(bf16[1024,896]{1,0:T(8,128)(2,1)S(1)} %bitcast.4), channel_id=1, source_target_pairs={{0,1},{1,0},{2,3},{3,2},{4,5},{5,4},{6,7},{7,6},{8,9},{9,8},{10,11... | collective-permute-start | bytes 5505032 | tf_op jit(solution)/shard_map/ppermute | solution.py:234
  68.3 3.1 %own.1 = (bf16[1024,1024]{1,0:T(8,128)(2,1)S(1)}, f32[1,1024]{1,0:T(1,128)S(1)}, f32[1,1024]{1,0:T(1,128)S(1)}) custom-call(bf16[1024,896]{1,0:T(8,128)(2,1)S(1)} %bitcast.5), custom_call_target="tpu_custom_call" | custom-call | tf_op jit(solution)/shard_map/own/pallas_call | solution.py:235
  71.5 0.3 collective-permute-done.got_ref
  71.8 3.2 %other.1 = f32[128,1,128]{2,1,0:T(1,128)S(1)} custom-call(bf16[1024,1024]{1,0:T(8,128)(2,1)S(1)} %get-tuple-element.11.own_ref, bf16[1024,896]{1,0:T(8,128)(2,1)S(1)} %collective-permute-done.got_ref, f32[1,1024]{1,0:T(1,128)S(1)} %get-tuple-element.12.peak_ref, f32[1,1024]{1,0:T(1,128)S(1)} %get-tuple-element.13.total_ref), custom_call_target="tpu_custom_call" | custom-call | tf_op jit(solution)/shard_map/other/pallas_call | solution.py:251
  74.9 16.1 %all_to_all.11.returned_ref = f32[128,1,128]{2,1,0:T(1,128)S(1)} all-to-all(f32[128,1,128]{2,1,0:T(1,128)S(1)} %other.1), channel_id=1, replica_groups=mesh['gx'=128,'gy'=2] {'gx'}, dimensions={0} | all-to-all | bytes 131072 | tf_op jit(solution)/shard_map/all_to_all | solution.py:263
  91.1 0.9 pick.1
Async XLA Ops:
  65.9 5.9 %collective-permute-start = (bf16[1024,896]{1,0:T(8,128)(2,1)S(1)}, bf16[1024,896]{1,0:T(8,128)(2,1)S(1)}, u32[]{:S(2)}, u32[]{:S(2)}) collective-permute-start(bf16[1024,896]{1,0:T(8,128)(2,1)S(1)} %bitcast.4), channel_id=1, source_target_pairs={{0,1},{1,0},{2,3},{3,2},{4,5},{5,4},{6,7},{7,6},{8,9},{9,8},{10,11... | collective-permute-start | bytes 5505032 | tf_op jit(solution)/shard_map/ppermute | solution.py:234

commit v6 on v5

--- a/solution.py
+++ b/solution.py
@@ -17,7 +17,7 @@
 LAST = SLOTS - 1
 SHARED = LANES // SLOTS
 BLOCK = 512
-PART = 512
+PARTS = (512, 256)
 COPIES = 1
 
 
@@ -114,9 +114,8 @@
     bias_ref[...] = jnp.where((lead > 0.75 * ABSENT) | (level == LAST), HIDDEN, 0.0)
 
 
-def score_part(key_ref, query_ref, bias_ref, scores_ref, n, part, own):
+def score_part(key_ref, query_ref, bias_ref, scores_ref, n, keys, own):
     width = key_ref.shape[1]
-    keys = slice(part * PART, (part + 1) * PART)
     lanes = slice(n * BLOCK, (n + 1) * BLOCK)
     if own:
         scores = dot_t(key_ref[keys, :], query_ref[lanes, :])
@@ -124,8 +123,8 @@
         scores = dot(key_ref[keys, :], query_ref[:, lanes])
     bias = jnp.concatenate([bias_ref[keys, :]] * (BLOCK // LANES), axis=1)
     scores = scores * (LOG2E * width**-0.5) + bias
-    if own and part * PART <= n * BLOCK < (part + 1) * PART:
-        me = iota(scores.shape, 0) == iota(scores.shape, 1) + (n * BLOCK - part * PART)
+    if own and keys.start < lanes.stop and lanes.start < keys.stop:
+        me = iota(scores.shape, 0) == iota(scores.shape, 1) + (lanes.start - keys.start)
         scores = jnp.where(me, HIDDEN, scores)
     scores_ref[n, keys, :] = scores
     return jnp.max(scores, axis=0, keepdims=True)
@@ -133,19 +132,20 @@
 
 def fold(key_ref, query_ref, bias_ref, scores_ref, own, before, finish):
     count = key_ref.shape[0]
-    blocks, parts = count // BLOCK, count // PART
+    blocks, size = count // BLOCK, PARTS[0 if own else 1]
+    parts = [slice(k, k + size) for k in range(0, count, size)]
     peaks, totals = {}, {}
     for n in range(blocks + 1):
         if n < blocks:
             peaks[n], totals[n] = before(n)
             old, new = peaks[n], peaks[n]
-        for part in range(parts):
+        for keys in parts:
             if n < blocks:
                 new = jnp.maximum(
-                    new, score_part(key_ref, query_ref, bias_ref, scores_ref, n, part, own)
+                    new, score_part(key_ref, query_ref, bias_ref, scores_ref, n, keys, own)
                 )
             if n > 0:
-                scores = scores_ref[n - 1, part * PART : (part + 1) * PART, :]
+                scores = scores_ref[n - 1, keys, :]
                 totals[n - 1] += jnp.sum(jnp.exp2(scores - peaks[n - 1]), axis=0, keepdims=True)
         if n < blocks:
             totals[n] = totals[n] * jnp.exp2(old - new)

time: 92.1 us -> 92 us (level)
  no operation moved by 1% of the time
where the time goes in v6:
time: 92 us; the launch traced here: 91.8 us
  blocking collectives  79.5 us (86%)
  Pallas kernels  9.5 us (10%)
  starting transfers between devices  2.47 us (3%)
    all_to_all x1, blocking collectives, shards(): lax.all_to_all(send.reshape(owners, SLOTS, main), 'gx', split_axis=0, con...  63.4 us
    all_to_all x1, blocking collectives, shards(): lax.all_to_all(density, 'gx', split_axis=0, concat_axis=0, tiled=True)  16.1 us
    pallas_call x1, Pallas kernels, shards(): pl.pallas_call(own_kernel, in_specs=[VMEM_SPEC], out_shape=(pltpu.VMEM((w...  3.14 us
    pallas_call x1, Pallas kernels, shards(): pl.pallas_call(other_kernel, in_specs=[VMEM_SPEC] * 4, out_shape=jax.Shap...  2.99 us
    pallas_call x1, Pallas kernels, shards(): pl.pallas_call(pack_kernel, in_specs=[ANY_SPEC, ANY_SPEC], out_shape=(jax...  2.48 us
    ppermute x1, starting transfers between devices, shards(): other = lax.ppermute(got, 'gy', [(0, 1), (1, 0)])  2.47 us
  transfers between devices with their start and end apart: 1, of which 1 were waited for; matrix products, arithmetic and copies ran while one was open for 0% of the time, Pallas kernels for 3%

profile of v6, /device:TPU:1, one launch (start us, length us, event | category | flops | bytes accessed | tf_op | source)
XLA Modules:
  0.0 91.8 jit_solution(4159062379042622417)
XLA Ops:
  0.0 2.5 %pack.1 = (bf16[1024,896]{1,0:T(8,128)(2,1)S(1)}, s32[1,448]{1,0:T(1,128)S(1)}) custom-call(s32[1,448]{1,0:T(1,128)} %bitcast.7, bf16[448,1024]{1,0:T(8,128)(2,1)} %rows_hbm.1), custom_call_target="tpu_custom_call" | custom-call | tf_op jit(solution)/shard_map/pack/pallas_call | solution.py:212
  2.5 63.4 %all_to_all.10 = bf16[128,8,896]{2,1,0:T(8,128)(2,1)S(1)} all-to-all(bf16[128,8,896]{2,1,0:T(8,128)(2,1)S(1)} %bitcast.6), channel_id=1, replica_groups=mesh['gx'=128,'gy'=2] {'gx'}, dimensions={0} | all-to-all | bytes 3670016 | tf_op jit(solution)/shard_map/all_to_all | solution.py:231
  65.9 2.5 %collective-permute-start = (bf16[1024,896]{1,0:T(8,128)(2,1)S(1)}, bf16[1024,896]{1,0:T(8,128)(2,1)S(1)}, u32[]{:S(2)}, u32[]{:S(2)}) collective-permute-start(bf16[1024,896]{1,0:T(8,128)(2,1)S(1)} %bitcast.4), channel_id=1, source_target_pairs={{0,1},{1,0},{2,3},{3,2},{4,5},{5,4},{6,7},{7,6},{8,9},{9,8},{10,11... | collective-permute-start | bytes 5505032 | tf_op jit(solution)/shard_map/ppermute | solution.py:234
  68.3 3.1 %own.1 = (bf16[1024,1024]{1,0:T(8,128)(2,1)S(1)}, f32[1,1024]{1,0:T(1,128)S(1)}, f32[1,1024]{1,0:T(1,128)S(1)}) custom-call(bf16[1024,896]{1,0:T(8,128)(2,1)S(1)} %bitcast.5), custom_call_target="tpu_custom_call" | custom-call | tf_op jit(solution)/shard_map/own/pallas_call | solution.py:235
  71.5 0.3 collective-permute-done.got_ref
  71.8 3.0 %other.1 = f32[128,1,128]{2,1,0:T(1,128)S(1)} custom-call(bf16[1024,1024]{1,0:T(8,128)(2,1)S(1)} %get-tuple-element.11.own_ref, bf16[1024,896]{1,0:T(8,128)(2,1)S(1)} %collective-permute-done.got_ref, f32[1,1024]{1,0:T(1,128)S(1)} %get-tuple-element.12.peak_ref, f32[1,1024]{1,0:T(1,128)S(1)} %get-tuple-element.13.total_ref), custom_call_target="tpu_custom_call" | custom-call | tf_op jit(solution)/shard_map/other/pallas_call | solution.py:251
  74.8 16.1 %all_to_all.11.returned_ref = f32[128,1,128]{2,1,0:T(1,128)S(1)} all-to-all(f32[128,1,128]{2,1,0:T(1,128)S(1)} %other.1), channel_id=1, replica_groups=mesh['gx'=128,'gy'=2] {'gx'}, dimensions={0} | all-to-all | bytes 131072 | tf_op jit(solution)/shard_map/all_to_all | solution.py:263
  90.9 0.9 pick.1
Async XLA Ops:
  65.9 5.9 %collective-permute-start = (bf16[1024,896]{1,0:T(8,128)(2,1)S(1)}, bf16[1024,896]{1,0:T(8,128)(2,1)S(1)}, u32[]{:S(2)}, u32[]{:S(2)}) collective-permute-start(bf16[1024,896]{1,0:T(8,128)(2,1)S(1)} %bitcast.4), channel_id=1, source_target_pairs={{0,1},{1,0},{2,3},{3,2},{4,5},{5,4},{6,7},{7,6},{8,9},{9,8},{10,11... | collective-permute-start | bytes 5505032 | tf_op jit(solution)/shard_map/ppermute | solution.py:234

commit v7 on v6

--- a/solution.py
+++ b/solution.py
@@ -103,7 +103,7 @@
     rest = jnp.zeros(shape, jnp.float32)
     for j in range(main // LANES):
         chunk = got_ref[:, chunk_of(j)].astype(jnp.float32).reshape(shape)
-        rest = jnp.where(level == j, pltpu.roll(chunk, (j - LAST) % SLOTS, 1), rest)
+        rest = jnp.where(level == j, jnp.broadcast_to(chunk[:, LAST:, :], shape), rest)
     full_ref[:, main:] = rest.reshape(count, LANES).astype(jnp.bfloat16)
 
 

time: 92 us -> 92 us (level)
  no operation moved by 1% of the time
where the time goes in v7:
time: 92 us; the launch traced here: 91.8 us
  blocking collectives  79.5 us (86%)
  Pallas kernels  9.51 us (10%)
  starting transfers between devices  2.47 us (3%)
    all_to_all x1, blocking collectives, shards(): lax.all_to_all(send.reshape(owners, SLOTS, main), 'gx', split_axis=0, con...  63.4 us
    all_to_all x1, blocking collectives, shards(): lax.all_to_all(density, 'gx', split_axis=0, concat_axis=0, tiled=True)  16.1 us
    pallas_call x1, Pallas kernels, shards(): pl.pallas_call(own_kernel, in_specs=[VMEM_SPEC], out_shape=(pltpu.VMEM((w...  3.13 us
    pallas_call x1, Pallas kernels, shards(): pl.pallas_call(other_kernel, in_specs=[VMEM_SPEC] * 4, out_shape=jax.Shap...  3.01 us
    pallas_call x1, Pallas kernels, shards(): pl.pallas_call(pack_kernel, in_specs=[ANY_SPEC, ANY_SPEC], out_shape=(jax...  2.48 us
    ppermute x1, starting transfers between devices, shards(): other = lax.ppermute(got, 'gy', [(0, 1), (1, 0)])  2.47 us
  transfers between devices with their start and end apart: 1, of which 1 were waited for; matrix products, arithmetic and copies ran while one was open for 0% of the time, Pallas kernels for 3%

profile of v7, /device:TPU:1, one launch (start us, length us, event | category | flops | bytes accessed | tf_op | source)
XLA Modules:
  0.0 91.8 jit_solution(10370858355868977943)
XLA Ops:
  0.0 2.5 %pack.1 = (bf16[1024,896]{1,0:T(8,128)(2,1)S(1)}, s32[1,448]{1,0:T(1,128)S(1)}) custom-call(s32[1,448]{1,0:T(1,128)} %bitcast.7, bf16[448,1024]{1,0:T(8,128)(2,1)} %rows_hbm.1), custom_call_target="tpu_custom_call" | custom-call | tf_op jit(solution)/shard_map/pack/pallas_call | solution.py:212
  2.5 63.4 %all_to_all.10 = bf16[128,8,896]{2,1,0:T(8,128)(2,1)S(1)} all-to-all(bf16[128,8,896]{2,1,0:T(8,128)(2,1)S(1)} %bitcast.6), channel_id=1, replica_groups=mesh['gx'=128,'gy'=2] {'gx'}, dimensions={0} | all-to-all | bytes 3670016 | tf_op jit(solution)/shard_map/all_to_all | solution.py:231
  65.9 2.5 %collective-permute-start = (bf16[1024,896]{1,0:T(8,128)(2,1)S(1)}, bf16[1024,896]{1,0:T(8,128)(2,1)S(1)}, u32[]{:S(2)}, u32[]{:S(2)}) collective-permute-start(bf16[1024,896]{1,0:T(8,128)(2,1)S(1)} %bitcast.4), channel_id=1, source_target_pairs={{0,1},{1,0},{2,3},{3,2},{4,5},{5,4},{6,7},{7,6},{8,9},{9,8},{10,11... | collective-permute-start | bytes 5505032 | tf_op jit(solution)/shard_map/ppermute | solution.py:234
  68.3 3.1 %own.1 = (bf16[1024,1024]{1,0:T(8,128)(2,1)S(1)}, f32[1,1024]{1,0:T(1,128)S(1)}, f32[1,1024]{1,0:T(1,128)S(1)}) custom-call(bf16[1024,896]{1,0:T(8,128)(2,1)S(1)} %bitcast.5), custom_call_target="tpu_custom_call" | custom-call | tf_op jit(solution)/shard_map/own/pallas_call | solution.py:235
  71.5 0.3 collective-permute-done.got_ref
  71.8 3.0 %other.1 = f32[128,1,128]{2,1,0:T(1,128)S(1)} custom-call(bf16[1024,1024]{1,0:T(8,128)(2,1)S(1)} %get-tuple-element.11.own_ref, bf16[1024,896]{1,0:T(8,128)(2,1)S(1)} %collective-permute-done.got_ref, f32[1,1024]{1,0:T(1,128)S(1)} %get-tuple-element.12.peak_ref, f32[1,1024]{1,0:T(1,128)S(1)} %get-tuple-element.13.total_ref), custom_call_target="tpu_custom_call" | custom-call | tf_op jit(solution)/shard_map/other/pallas_call | solution.py:251
  74.8 16.1 %all_to_all.11.returned_ref = f32[128,1,128]{2,1,0:T(1,128)S(1)} all-to-all(f32[128,1,128]{2,1,0:T(1,128)S(1)} %other.1), channel_id=1, replica_groups=mesh['gx'=128,'gy'=2] {'gx'}, dimensions={0} | all-to-all | bytes 131072 | tf_op jit(solution)/shard_map/all_to_all | solution.py:263
  90.9 0.9 pick.1
Async XLA Ops:
  65.9 5.9 %collective-permute-start = (bf16[1024,896]{1,0:T(8,128)(2,1)S(1)}, bf16[1024,896]{1,0:T(8,128)(2,1)S(1)}, u32[]{:S(2)}, u32[]{:S(2)}) collective-permute-start(bf16[1024,896]{1,0:T(8,128)(2,1)S(1)} %bitcast.4), channel_id=1, source_target_pairs={{0,1},{1,0},{2,3},{3,2},{4,5},{5,4},{6,7},{7,6},{8,9},{9,8},{10,11... | collective-permute-start | bytes 5505032 | tf_op jit(solution)/shard_map/ppermute | solution.py:234

commit v8 on v7

--- a/solution.py
+++ b/solution.py
@@ -91,7 +91,7 @@
             if j == 0:
                 empty = level.astype(jnp.float32) >= jnp.broadcast_to(members, level.shape)
                 chunk = jnp.where(empty & (iota(level.shape, 2) == 0), ABSENT, chunk)
-            chunk = jnp.where(level == LAST, pltpu.roll(rest, (LAST - j) % SLOTS, 1), chunk)
+            chunk = jnp.where(level == LAST, jnp.broadcast_to(rest[:, j : j + 1, :], level.shape), chunk)
             send_ref[:, chunk_of(j)] = chunk.reshape(count, LANES).astype(jnp.bfloat16)
 
 

time: 92 us -> 92 us (level)
  no operation moved by 1% of the time
where the time goes in v8:
time: 92 us; the launch traced here: 91.8 us
  blocking collectives  79.5 us (86%)
  Pallas kernels  9.53 us (10%)
  starting transfers between devices  2.47 us (3%)
    all_to_all x1, blocking collectives, shards(): lax.all_to_all(send.reshape(owners, SLOTS, main), 'gx', split_axis=0, con...  63.4 us
    all_to_all x1, blocking collectives, shards(): lax.all_to_all(density, 'gx', split_axis=0, concat_axis=0, tiled=True)  16.1 us
    pallas_call x1, Pallas kernels, shards(): pl.pallas_call(own_kernel, in_specs=[VMEM_SPEC], out_shape=(pltpu.VMEM((w...  3.13 us
    pallas_call x1, Pallas kernels, shards(): pl.pallas_call(other_kernel, in_specs=[VMEM_SPEC] * 4, out_shape=jax.Shap...  3.01 us
    pallas_call x1, Pallas kernels, shards(): pl.pallas_call(pack_kernel, in_specs=[ANY_SPEC, ANY_SPEC], out_shape=(jax...  2.49 us
    ppermute x1, starting transfers between devices, shards(): other = lax.ppermute(got, 'gy', [(0, 1), (1, 0)])  2.47 us
  transfers between devices with their start and end apart: 1, of which 1 were waited for; matrix products, arithmetic and copies ran while one was open for 0% of the time, Pallas kernels for 3%

profile of v8, /device:TPU:1, one launch (start us, length us, event | category | flops | bytes accessed | tf_op | source)
XLA Modules:
  0.0 91.8 jit_solution(7719622121676374033)
XLA Ops:
  0.0 2.5 %pack.1 = (bf16[1024,896]{1,0:T(8,128)(2,1)S(1)}, s32[1,448]{1,0:T(1,128)S(1)}) custom-call(s32[1,448]{1,0:T(1,128)} %bitcast.7, bf16[448,1024]{1,0:T(8,128)(2,1)} %rows_hbm.1), custom_call_target="tpu_custom_call" | custom-call | tf_op jit(solution)/shard_map/pack/pallas_call | solution.py:212
  2.5 63.4 %all_to_all.10 = bf16[128,8,896]{2,1,0:T(8,128)(2,1)S(1)} all-to-all(bf16[128,8,896]{2,1,0:T(8,128)(2,1)S(1)} %bitcast.6), channel_id=1, replica_groups=mesh['gx'=128,'gy'=2] {'gx'}, dimensions={0} | all-to-all | bytes 3670016 | tf_op jit(solution)/shard_map/all_to_all | solution.py:231
  65.9 2.5 %collective-permute-start = (bf16[1024,896]{1,0:T(8,128)(2,1)S(1)}, bf16[1024,896]{1,0:T(8,128)(2,1)S(1)}, u32[]{:S(2)}, u32[]{:S(2)}) collective-permute-start(bf16[1024,896]{1,0:T(8,128)(2,1)S(1)} %bitcast.4), channel_id=1, source_target_pairs={{0,1},{1,0},{2,3},{3,2},{4,5},{5,4},{6,7},{7,6},{8,9},{9,8},{10,11... | collective-permute-start | bytes 5505032 | tf_op jit(solution)/shard_map/ppermute | solution.py:234
  68.4 3.1 %own.1 = (bf16[1024,1024]{1,0:T(8,128)(2,1)S(1)}, f32[1,1024]{1,0:T(1,128)S(1)}, f32[1,1024]{1,0:T(1,128)S(1)}) custom-call(bf16[1024,896]{1,0:T(8,128)(2,1)S(1)} %bitcast.5), custom_call_target="tpu_custom_call" | custom-call | tf_op jit(solution)/shard_map/own/pallas_call | solution.py:235
  71.5 0.3 collective-permute-done.got_ref
  71.8 3.0 %other.1 = f32[128,1,128]{2,1,0:T(1,128)S(1)} custom-call(bf16[1024,1024]{1,0:T(8,128)(2,1)S(1)} %get-tuple-element.11.own_ref, bf16[1024,896]{1,0:T(8,128)(2,1)S(1)} %collective-permute-done.got_ref, f32[1,1024]{1,0:T(1,128)S(1)} %get-tuple-element.12.peak_ref, f32[1,1024]{1,0:T(1,128)S(1)} %get-tuple-element.13.total_ref), custom_call_target="tpu_custom_call" | custom-call | tf_op jit(solution)/shard_map/other/pallas_call | solution.py:251
  74.8 16.1 %all_to_all.11.returned_ref = f32[128,1,128]{2,1,0:T(1,128)S(1)} all-to-all(f32[128,1,128]{2,1,0:T(1,128)S(1)} %other.1), channel_id=1, replica_groups=mesh['gx'=128,'gy'=2] {'gx'}, dimensions={0} | all-to-all | bytes 131072 | tf_op jit(solution)/shard_map/all_to_all | solution.py:263
  90.9 0.9 pick.1
Async XLA Ops:
  65.9 5.9 %collective-permute-start = (bf16[1024,896]{1,0:T(8,128)(2,1)S(1)}, bf16[1024,896]{1,0:T(8,128)(2,1)S(1)}, u32[]{:S(2)}, u32[]{:S(2)}) collective-permute-start(bf16[1024,896]{1,0:T(8,128)(2,1)S(1)} %bitcast.4), channel_id=1, source_target_pairs={{0,1},{1,0},{2,3},{3,2},{4,5},{5,4},{6,7},{7,6},{8,9},{9,8},{10,11... | collective-permute-start | bytes 5505032 | tf_op jit(solution)/shard_map/ppermute | solution.py:234

commit v9 on v7

--- a/solution.py
+++ b/solution.py
@@ -199,7 +199,8 @@
     left = turned - high.astype(jnp.float32)
     middle = left.astype(jnp.bfloat16)
     low = (left - middle.astype(jnp.float32)).astype(jnp.bfloat16)
-    picked = (dot(low, named) + dot(middle, named)) + dot(high, named)
+    thirds = dot(jnp.concatenate([low, middle, high], axis=0), named)
+    picked = (thirds[:SLOTS] + thirds[SLOTS : 2 * SLOTS]) + thirds[2 * SLOTS :]
     mine = iota((SLOTS, count), 0) == slot % SLOTS
     density_ref[...] = jnp.sum(jnp.where(mine, picked, 0.0), axis=0, keepdims=True)
 

time: 92 us -> 91.9 us (level)
  no operation moved by 1% of the time
where the time goes in v9:
time: 91.9 us; the launch traced here: 91.8 us
  blocking collectives  79.5 us (87%)
  Pallas kernels  9.49 us (10%)
  starting transfers between devices  2.47 us (3%)
    all_to_all x1, blocking collectives, shards(): lax.all_to_all(send.reshape(owners, SLOTS, main), 'gx', split_axis=0, con...  63.4 us
    all_to_all x1, blocking collectives, shards(): lax.all_to_all(density, 'gx', split_axis=0, concat_axis=0, tiled=True)  16.1 us
    pallas_call x1, Pallas kernels, shards(): pl.pallas_call(own_kernel, in_specs=[VMEM_SPEC], out_shape=(pltpu.VMEM((w...  3.13 us
    pallas_call x1, Pallas kernels, shards(): pl.pallas_call(other_kernel, in_specs=[VMEM_SPEC] * 4, out_shape=jax.Shap...  3.01 us
    pallas_call x1, Pallas kernels, shards(): pl.pallas_call(pack_kernel, in_specs=[ANY_SPEC, ANY_SPEC], out_shape=(jax...  2.48 us
    ppermute x1, starting transfers between devices, shards(): other = lax.ppermute(got, 'gy', [(0, 1), (1, 0)])  2.47 us
  transfers between devices with their start and end apart: 1, of which 1 were waited for; matrix products, arithmetic and copies ran while one was open for 0% of the time, Pallas kernels for 3%

profile of v9, /device:TPU:1, one launch (start us, length us, event | category | flops | bytes accessed | tf_op | source)
XLA Modules:
  0.0 91.8 jit_solution(7763742784191366772)
XLA Ops:
  0.0 2.5 %pack.1 = (bf16[1024,896]{1,0:T(8,128)(2,1)S(1)}, s32[1,448]{1,0:T(1,128)S(1)}) custom-call(s32[1,448]{1,0:T(1,128)} %bitcast.7, bf16[448,1024]{1,0:T(8,128)(2,1)} %rows_hbm.1), custom_call_target="tpu_custom_call" | custom-call | tf_op jit(solution)/shard_map/pack/pallas_call | solution.py:213
  2.5 63.4 %all_to_all.10 = bf16[128,8,896]{2,1,0:T(8,128)(2,1)S(1)} all-to-all(bf16[128,8,896]{2,1,0:T(8,128)(2,1)S(1)} %bitcast.6), channel_id=1, replica_groups=mesh['gx'=128,'gy'=2] {'gx'}, dimensions={0} | all-to-all | bytes 3670016 | tf_op jit(solution)/shard_map/all_to_all | solution.py:232
  65.9 2.5 %collective-permute-start = (bf16[1024,896]{1,0:T(8,128)(2,1)S(1)}, bf16[1024,896]{1,0:T(8,128)(2,1)S(1)}, u32[]{:S(2)}, u32[]{:S(2)}) collective-permute-start(bf16[1024,896]{1,0:T(8,128)(2,1)S(1)} %bitcast.4), channel_id=1, source_target_pairs={{0,1},{1,0},{2,3},{3,2},{4,5},{5,4},{6,7},{7,6},{8,9},{9,8},{10,11... | collective-permute-start | bytes 5505032 | tf_op jit(solution)/shard_map/ppermute | solution.py:235
  68.3 3.1 %own.1 = (bf16[1024,1024]{1,0:T(8,128)(2,1)S(1)}, f32[1,1024]{1,0:T(1,128)S(1)}, f32[1,1024]{1,0:T(1,128)S(1)}) custom-call(bf16[1024,896]{1,0:T(8,128)(2,1)S(1)} %bitcast.5), custom_call_target="tpu_custom_call" | custom-call | tf_op jit(solution)/shard_map/own/pallas_call | solution.py:236
  71.5 0.3 collective-permute-done.got_ref
  71.8 3.0 %other.1 = f32[128,1,128]{2,1,0:T(1,128)S(1)} custom-call(bf16[1024,1024]{1,0:T(8,128)(2,1)S(1)} %get-tuple-element.11.own_ref, bf16[1024,896]{1,0:T(8,128)(2,1)S(1)} %collective-permute-done.got_ref, f32[1,1024]{1,0:T(1,128)S(1)} %get-tuple-element.12.peak_ref, f32[1,1024]{1,0:T(1,128)S(1)} %get-tuple-element.13.total_ref), custom_call_target="tpu_custom_call" | custom-call | tf_op jit(solution)/shard_map/other/pallas_call | solution.py:252
  74.8 16.1 %all_to_all.11.returned_ref = f32[128,1,128]{2,1,0:T(1,128)S(1)} all-to-all(f32[128,1,128]{2,1,0:T(1,128)S(1)} %other.1), channel_id=1, replica_groups=mesh['gx'=128,'gy'=2] {'gx'}, dimensions={0} | all-to-all | bytes 131072 | tf_op jit(solution)/shard_map/all_to_all | solution.py:264
  90.9 0.9 pick.1
Async XLA Ops:
  65.9 5.9 %collective-permute-start = (bf16[1024,896]{1,0:T(8,128)(2,1)S(1)}, bf16[1024,896]{1,0:T(8,128)(2,1)S(1)}, u32[]{:S(2)}, u32[]{:S(2)}) collective-permute-start(bf16[1024,896]{1,0:T(8,128)(2,1)S(1)} %bitcast.4), channel_id=1, source_target_pairs={{0,1},{1,0},{2,3},{3,2},{4,5},{5,4},{6,7},{7,6},{8,9},{9,8},{10,11... | collective-permute-start | bytes 5505032 | tf_op jit(solution)/shard_map/ppermute | solution.py:235
